TPU v7x, 256 devices: a whole 4x4x8 slice. The times are simulated.
256 devices in a mesh: wheel: 32 (over x_hi, z, core), slab: 8 (over x_lo, y).
Axes of the slice: x: 4 (x_hi: 2, x_lo: 2; x = x_hi * 2 + x_lo), y: 4, z: 8, core: 2. Of those that a mesh axis runs over, the one named last changes fastest.
Arguments:
- krylov_block: float32 [2, 64, 3, 16, 2048], P(None, 'wheel', None, None, 'slab'), may hold values from -6 to 6
- blade_class: int32 [64], P('wheel'), may hold values from 0 to 3
- neighbors: int32 [8, 2048], P(None, 'slab'), may hold values from 0 to 511
- iface_rows: int32 [2, 512], P(None, 'slab'), may hold values from 0 to 255
- face_rows: int32 [2, 512], P(None, 'slab'), may hold values from 0 to 255
- stiffness: float32 [3, 3, 8, 2048], P(None, None, None, 'slab'), may hold values from -1.25 to 1.25
- lumped_mass: float32 [3, 2048], P(None, 'slab'), may hold values from 0.5 to 2
- precond: bfloat16 [32, 64, 384, 384], P('wheel', 'slab'), may hold values from -0.3125 to 0.3125
Outputs:
- preconditioned: float32 [32, 64, 16, 384], P('wheel', 'slab')
Inputs may be any that keep to these rules, and one draw needn't show every extreme that they name: `neighbors`: extended numbering: own nodes first (256), then 64 from the lower slab, 64 from the upper slab, 64 from the previous sector, 64 from the next sector.
All inputs are finite; a program needn't handle non-finite values.
Results may differ from a plain program's by a relative error of at most 0.0039.
Values may be sent and summed in bfloat16 or wider, within the bound.
A program may use at most 64 MiB of HBM per device.

v0:
```python
import math

import jax
import jax.numpy as jnp
from jax import lax
from jax.sharding import PartitionSpec as P

GROUP = 32


damping_ratio = 0.5
gyro_rate = 0.8
shift_value = 0.3
class_step = 0.125


def extended_2(block, sides, width, periodic):
    for axis, dim in sides:
        count = lax.axis_size(axis)
        forward = [(i, i + 1) for i in range(count - 1)]
        if periodic:
            forward.append((count - 1, 0))
        backward = [(target, source) for source, target in forward]
        low = lax.ppermute(
            lax.slice_in_dim(block, block.shape[dim] - width, None, axis=dim), axis, forward
        )
        high = lax.ppermute(lax.slice_in_dim(block, 0, width, axis=dim), axis, backward)
        block = jnp.concatenate([low, block, high], axis=dim)
    return block


def basis(row_ids, col_ids, sectors_all):
    pair_id = row_ids[:, None] // 2
    part_id = row_ids[:, None] % 2
    sector_id = col_ids[None, :]
    phases = pair_id * sector_id % sectors_all
    angles = 2.0 * math.pi / sectors_all * phases.astype(jnp.float32)
    parity = (1 - 2 * (sector_id % 2)).astype(jnp.float32)
    edge_rows = jnp.where(
        part_id == 0, jnp.ones_like(angles), parity * jnp.ones_like(angles)
    ) * math.sqrt(1.0 / sectors_all)
    inner_rows = jnp.where(part_id == 0, jnp.cos(angles), jnp.sin(angles)) * math.sqrt(
        2.0 / sectors_all
    )
    return jnp.where(pair_id == 0, edge_rows, inner_rows)


def arrange(harmonic):
    pair_rows, states, comps, vectors, nodes = harmonic.shape
    shaped = harmonic.reshape(pair_rows // 2, 2, states, comps, vectors, nodes // GROUP, GROUP)
    shaped = shaped.transpose(0, 5, 4, 1, 2, 3, 6)
    return shaped.reshape(pair_rows // 2, nodes // GROUP, vectors, 4 * comps * GROUP)


def on_device(
    krylov_block, blade_class, neighbors, iface_rows, face_rows, stiffness, lumped_mass, precond
):
    displacement = krylov_block[0]
    velocity = krylov_block[1]
    moved_field = displacement + damping_ratio * velocity
    rim_width = iface_rows.shape[1]
    face_width = face_rows.shape[1]
    rims = jnp.concatenate(
        (
            jnp.take(moved_field, iface_rows[0], axis=3),
            jnp.take(moved_field, iface_rows[1], axis=3),
        ),
        axis=3,
    )
    rimmed = extended_2(rims.astype(jnp.bfloat16), (("slab", 3),), rim_width, False).astype(
        rims.dtype
    )
    from_lower = rimmed[..., :rim_width]
    from_upper = rimmed[..., 3 * rim_width :]
    left_face = jnp.take(moved_field, face_rows[0], axis=3)
    right_face = jnp.take(moved_field, face_rows[1], axis=3)
    edges = jnp.concatenate((left_face[0], right_face[-1]), axis=2)
    faced = extended_2(edges, (("wheel", 2),), face_width, True)
    from_prev = jnp.concatenate((faced[None, :, :, :face_width], right_face[:-1]), axis=0)
    from_next = jnp.concatenate((left_face[1:], faced[None, :, :, 3 * face_width :]), axis=0)
    extended = jnp.concatenate((moved_field, from_lower, from_upper, from_prev, from_next), axis=3)
    picked = jnp.take(extended, neighbors, axis=3)
    restore = jnp.einsum("cdkn,sdvkn->scvn", stiffness, picked, precision=lax.Precision.HIGHEST)
    scale = (1.0 + class_step * blade_class.astype(jnp.float32))[:, None, None, None]
    gyro = gyro_rate * jnp.stack(
        (
            -lumped_mass[0] * velocity[:, 1],
            lumped_mass[1] * velocity[:, 0],
            jnp.zeros_like(velocity[:, 2]),
        ),
        axis=1,
    )
    res_disp = velocity - shift_value * displacement
    res_velo = -scale * restore - gyro - shift_value * lumped_mass[None, :, None, :] * velocity
    residual = jnp.stack((res_disp, res_velo), axis=0)
    local_sectors = residual.shape[1]
    sectors_all = lax.axis_size("wheel") * local_sectors
    offset = lax.axis_index("wheel") * local_sectors
    table = basis(
        jnp.arange(local_sectors * lax.axis_size("wheel"), dtype=jnp.int32),
        offset + jnp.arange(local_sectors, dtype=jnp.int32),
        sectors_all,
    )
    summed = lax.psum_scatter(
        jnp.einsum("bs,tscvn->btcvn", table, residual, precision=lax.Precision.HIGHEST),
        "wheel",
        scatter_dimension=0,
        tiled=True,
    )
    harmonic = summed.astype(jnp.bfloat16)
    lhs = arrange(harmonic)
    return jnp.einsum("pgvj,pgij->pgvi", lhs, precond, preferred_element_type=jnp.float32)


def solution(mesh):
    return jax.shard_map(
        on_device,
        mesh=mesh,
        in_specs=(
            P(None, "wheel", None, None, "slab"),
            P("wheel"),
            P(None, "slab"),
            P(None, "slab"),
            P(None, "slab"),
            P(None, None, None, "slab"),
            P(None, "slab"),
            P("wheel", "slab", None, None),
        ),
        out_specs=P("wheel", "slab", None, None),
        check_vma=False,
    )
```

profile of v0, /device:TPU:1, one launch (start us, length us, event | category | flops | bytes accessed | tf_op | source)
XLA Modules:
  0.0 235.3 jit_solution(12764242699975857736)
XLA Ops:
  6.5 0.9 compare_and_fusion.4
  7.4 1.0 bitcast_add_fusion
  8.4 0.5 copy.138
  8.8 0.8 gather_fusion.2
  9.7 0.1 copy.141
  9.8 1.3 collective-permute-start.1
  11.1 0.8 gather_fusion.1
  11.9 0.1 copy.139
  12.0 5.3 %collective-permute-start = (bf16[2,3,16,64]{3,2,1,0:T(8,128)(2,1)S(1)}, bf16[2,3,16,64]{3,2,1,0:T(8,128)(2,1)}, u32[]{:S(2)}, u32[]{:S(2)}) collective-permute-start(bf16[2,3,16,64]{3,2,1,0:T(8,128)(2,1)S(1)} %bitcast_convert_fusion.1), channel_id=1, source_target_pairs={{0,1},{1,2},{2,3},{3,4},{4,5},{5,6},{6,7},{8,9},{9,10},{10,11},{11... | collective-permute-start | bytes 36872 | tf_op jit(solution)/shard_map/ppermute | solution.py:24
  17.3 0.8 compare_and_fusion.1
  18.1 0.8 gather_fusion.4
  18.9 1.5 gather_fusion.3
  20.4 1.0 copy.143
  21.4 0.1 copy.145
  21.6 3.2 %collective-permute-start.3 = (f32[3,16,64]{2,1,0:T(8,128)S(1)}, f32[3,16,64]{2,1,0:T(8,128)S(1)}, u32[]{:S(2)}, u32[]{:S(2)}) collective-permute-start(f32[3,16,64]{2,1,0:T(8,128)S(1)} %get-tuple-element.21), channel_id=1, source_target_pairs={{8,0},{16,8},{24,16},{32,24},{40,32},{48,40},{56,48},{64,56},{72,6... | collective-permute-start | bytes 36872 | tf_op jit(solution)/shard_map/ppermute | solution.py:27
  24.8 0.0 collective-permute-start.2
  24.8 0.8 slice_negate_fusion
  25.6 0.7 broadcast_multiply_fusion
  26.3 0.7 compare_and_fusion
  27.0 0.7 fusion.17
  27.7 1.6 multiply_subtract_fusion
  29.3 1.2 add_negate_fusion
  30.5 0.5 fusion.35
  31.0 0.6 slice_multiply_fusion.1
  31.6 0.6 and_select_fusion.3
  32.2 0.2 copy.137
  32.4 2.2 copy.153
  34.6 0.6 pad.4.clone
  35.2 0.9 maximum_convert_fusion
  36.1 0.1 fusion.55
  36.1 0.0 collective-permute-done.3
  36.2 0.0 collective-permute-done.2
  36.2 0.1 concatenate.18
  36.3 2.1 copy.146
  38.4 23.2 %gather_fusion = f32[2048,2,3,16]{3,1,2,0:T(2,128)} fusion(f32[2,3,16,512]{2,0,3,1:T(2,128)} %copy.146, s32[2048]{0:T(1024)S(1)} %broadcast_clamp_fusion), kind=kCustom, calls=%fused_computation.4 | custom fusion | bytes 1581056 | tf_op jit(solution)/shard_map/jit(_take)/gather | solution.py:82
  61.6 10.7 %fusion.6 = f32[256,2,16,3]{2,3,1,0:T(4,128)S(1)} fusion(f32[3,3,8,256,1]{2,0,1,4,3:T(4,128)} %copy.153, f32[8,256,2,3,16]{4,2,3,1,0:T(2,128)} %bitcast.73, pred[8,256]{0,1:T(8,128)(4,1)S(1)} %copy.137), kind=kOutput, calls=%fused_computation.12 | convolution fusion | flops 7274496 | bytes 960512 | tf_op jit(solution)/shard_map/cdkn,sdvkn->scvn/dot_general | solution.py:83
  72.3 0.4 copy.149
  72.7 1.0 fusion.16
  73.7 0.9 pad_maximum_fusion
  74.7 6.3 %fusion.12 = f32[64,2,3,16,256]{4,0,3,2,1:T(8,128)S(1)} fusion(f32[2,2,3,16,256]{4,3,2,1,0:T(8,128)S(1)} %pad_maximum_fusion, pred[64]{0:T(512)(128)(4,1)S(1)} %get-tuple-element.34, pred[64]{0:T(512)(128)(4,1)S(1)} %get-tuple-element.35, s32[64]{0:T(128)} %and_select_fusion.3, s32[2]{0:T(128)} %get-tuple-element.33, f32[2]{0:T(128)S(1)} %get-tuple-element.32), kind=kOutput, calls=%fused_computation.16 | convolution fusion | flops 37751168 | bytes 6488464 | tf_op jit(solution)/shard_map/bs,tscvn->btcvn/dot_general | solution.py:105
  80.9 6.3 %copy.151 = f32[64,2,3,16,256]{4,3,2,1,0:T(8,128)} copy(f32[64,2,3,16,256]{4,0,3,2,1:T(8,128)S(1)} %fusion.12) | data formatting | bytes 12582912 | tf_op jit(solution)/shard_map/bs,tscvn->btcvn/dot_general | solution.py:105
  87.2 0.0 reduce-scatter.2.cloned.1.call-update
  87.3 137.9 %reduce-scatter.2.cloned.1.call-done = f32[2,2,3,16,256]{4,3,2,1,0:T(8,128)} async-done(((f32[64,2,3,16,256]{4,3,2,1,0:T(8,128)}), f32[2,2,3,16,256]{4,3,2,1,0:T(8,128)}) %reduce-scatter.2.cloned.1.call-update) | async-done | bytes 196624 | tf_op jit(solution)/shard_map/reduce_scatter | solution.py:104
  225.1 0.9 convert_element_type.25
  226.1 0.2 reshape.119
  226.3 0.3 copy.168
  226.6 0.3 reshape.120
  226.9 1.5 fusion.9
  (19 shorter events, 0.1 us)
Async XLA Ops:
  6.5 220.4 %copy-start = (bf16[1,8,384,384]{3,2,1,0:T(8,128)(2,1)S(1)}, bf16[1,8,384,384]{3,2,1,0:T(8,128)(2,1)}, u32[]{:S(2)}) copy-start(bf16[1,8,384,384]{3,2,1,0:T(8,128)(2,1)} %param.17) | copy-start | bytes 7077892
  6.5 218.6 %reduce-scatter.2.cloned.1.call-start = ((), (), s32[]{:S(2)}) async-start(), calls=%async_computation.1 | async-start | bytes 6488064 | tf_op jit(solution)/shard_map/reduce_scatter | solution.py:104
  9.8 25.4 %collective-permute-start.1 = (bf16[2,3,16,64]{3,2,1,0:T(8,128)(2,1)S(1)}, bf16[2,3,16,64]{3,2,1,0:T(8,128)(2,1)}, u32[]{:S(2)}, u32[]{:S(2)}) collective-permute-start(bf16[2,3,16,64]{3,2,1,0:T(8,128)(2,1)S(1)} %bitcast_convert_fusion), channel_id=1, source_target_pairs={{1,0},{2,1},{3,2},{4,3},{5,4},{6,5},{7,6},{9,8},{10,9},{11,10},{12... | collective-permute-start | bytes 36872 | tf_op jit(solution)/shard_map/ppermute | solution.py:27
  12.0 23.2 %collective-permute-start = (bf16[2,3,16,64]{3,2,1,0:T(8,128)(2,1)S(1)}, bf16[2,3,16,64]{3,2,1,0:T(8,128)(2,1)}, u32[]{:S(2)}, u32[]{:S(2)}) collective-permute-start(bf16[2,3,16,64]{3,2,1,0:T(8,128)(2,1)S(1)} %bitcast_convert_fusion.1), channel_id=1, source_target_pairs={{0,1},{1,2},{2,3},{3,4},{4,5},{5,6},{6,7},{8,9},{9,10},{10,11},{11... | collective-permute-start | bytes 36872 | tf_op jit(solution)/shard_map/ppermute | solution.py:24
  21.6 14.5 %collective-permute-start.3 = (f32[3,16,64]{2,1,0:T(8,128)S(1)}, f32[3,16,64]{2,1,0:T(8,128)S(1)}, u32[]{:S(2)}, u32[]{:S(2)}) collective-permute-start(f32[3,16,64]{2,1,0:T(8,128)S(1)} %get-tuple-element.21), channel_id=1, source_target_pairs={{8,0},{16,8},{24,16},{32,24},{40,32},{48,40},{56,48},{64,56},{72,6... | collective-permute-start | bytes 36872 | tf_op jit(solution)/shard_map/ppermute | solution.py:27
  24.8 11.4 %collective-permute-start.2 = (f32[3,16,64]{2,1,0:T(8,128)S(1)}, f32[3,16,64]{2,1,0:T(8,128)S(1)}, u32[]{:S(2)}, u32[]{:S(2)}) collective-permute-start(f32[3,16,64]{2,1,0:T(8,128)S(1)} %get-tuple-element.22), channel_id=1, source_target_pairs={{0,8},{8,16},{16,24},{24,32},{32,40},{40,48},{48,56},{56,64},{64,7... | collective-permute-start | bytes 36872 | tf_op jit(solution)/shard_map/ppermute | solution.py:24
Sparse Core Ops, SparseCore 0:
  87.4 137.6 reduce-scatter.1
where the time goes:
time: 239 us; the launch traced here: 235 us
  waiting for transfers between devices  138 us (58%)
  local copies, waits for them, and re-layouts  41.8 us (17%)
  matrix products  18.5 us (8%)
  other arithmetic  13.8 us (6%)
  between operations  13.6 us (6%)
  starting transfers between devices  9.77 us (4%)
    reduce_scatter x1, waiting for transfers between devices, on_device(): lax.psum_scatter(jnp.einsum('bs,tscvn->btcvn', table, residual, precision...  138 us
    gather x1, local copies, waits for them, and re-layouts, on_device(): picked = jnp.take(extended, neighbors, axis=3)  23.2 us
    dot_general x1, matrix products, on_device(): jnp.einsum('cdkn,sdvkn->scvn', stiffness, picked, precision=lax.Precision...  10.7 us
    dot_general x1, local copies, waits for them, and re-layouts, on_device(): jnp.einsum('bs,tscvn->btcvn', table, residual, precision=lax.Precision.HI...  6.31 us
    dot_general x1, matrix products, on_device(): jnp.einsum('bs,tscvn->btcvn', table, residual, precision=lax.Precision.HI...  6.26 us
    ppermute x2, starting transfers between devices, extended_2(): lax.ppermute(lax.slice_in_dim(block, block.shape[dim] - width, None, axis...  5.27 us
  transfers between devices with their start and end apart: 5, of which 1 were waited for; matrix products, arithmetic and copies ran while one was open for 7% of the time, Pallas kernels for 0%

commit v1 on v0

v1 whole, which is shorter than its diff:
```python
import math

import jax
import jax.numpy as jnp
import numpy as np
from jax import lax
from jax.experimental import pallas as pl
from jax.experimental.pallas import tpu as pltpu
from jax.sharding import PartitionSpec as P

import ml_dtypes

damping_ratio = 0.5
gyro_rate = 0.8
shift_value = 0.3
class_step = 0.125

SECT = 64
WHEEL = 32
SLAB = 8
MESH = pl.DeviceIdType.MESH
BF = jnp.bfloat16
F32 = jnp.float32


def basis_table():
    b = np.arange(SECT)[:, None]
    s = np.arange(SECT)[None, :]
    p, q = b // 2, b % 2
    angle = 2.0 * math.pi / SECT * ((p * s) % SECT)
    inner = np.where(q == 0, np.cos(angle), np.sin(angle)) * math.sqrt(2.0 / SECT)
    edge = np.where(q == 0, 1.0, 1.0 - 2.0 * (s % 2)) * math.sqrt(1.0 / SECT)
    return np.where(p == 0, edge, inner).astype(np.float32)


def kron_table():
    full = np.kron(basis_table(), np.eye(8, dtype=np.float32))
    high = full.astype(ml_dtypes.bfloat16)
    low = (full - high.astype(np.float32)).astype(ml_dtypes.bfloat16)
    return np.stack((high, low))


def one_hot(rows, cols, index_row):
    at = lax.broadcasted_iota(jnp.int32, (rows, cols), 0)
    return jnp.where(at == index_row, 1.0, 0.0).astype(BF)


def kernel(
    kb, bc, nb, ifr, fcr, st, ms, pc_hbm, km_hbm, out,
    pcv, kmv, hs, hsw, hr, hrw, sb, rv1, sb2, rv2,
    lsem, hsend, hrecv, ssem1, rsem1, ssem2, rsem2,
):
    w = lax.axis_index("wheel")
    j = lax.axis_index("slab")

    barrier = pltpu.get_barrier_semaphore()

    @pl.loop(1, WHEEL)
    def _(i):
        pl.semaphore_signal(
            barrier, inc=1, device_id={"wheel": lax.rem(w + i, WHEEL)}, device_id_type=MESH
        )

    up = lax.rem(j + 1, SLAB)
    down = lax.rem(j + SLAB - 1, SLAB)
    nxt = lax.rem(w + 1, WHEEL)
    prv = lax.rem(w + WHEEL - 1, WHEEL)
    for slab in (up, down):
        pl.semaphore_signal(barrier, inc=1, device_id={"slab": slab}, device_id_type=MESH)

    copy_km = pltpu.make_async_copy(km_hbm, kmv, lsem.at[0])
    copy_pc = pltpu.make_async_copy(pc_hbm, pcv, lsem.at[1])
    copy_km.start()
    copy_pc.start()

    u = kb[0]
    v = kb[1]
    e = (u + damping_ratio * v).reshape(96, 256)
    ehi = e.astype(BF)
    elo = (e - ehi.astype(F32)).astype(BF)

    none = jnp.full((1, 64), -1, jnp.int32)
    index = jnp.concatenate(
        (ifr[1:2, :], none, none, ifr[0:1, :], fcr[1:2, :], none, none, fcr[0:1, :]), axis=1
    )
    picks = jnp.dot(ehi, one_hot(256, 512, index), preferred_element_type=F32)
    hs[0] = picks[:, 0:128].astype(BF)
    hs[1] = picks[:, 128:256].astype(BF)
    hsw[0] = picks[48:96, 256:384].astype(BF)
    hsw[1] = picks[0:48, 384:512].astype(BF)

    pl.semaphore_wait(barrier, WHEEL + 1)

    halos = [
        pltpu.make_async_remote_copy(
            src_ref=src, dst_ref=dst, send_sem=hsend.at[n], recv_sem=hrecv.at[n],
            device_id=to, device_id_type=MESH,
        )
        for n, (src, dst, to) in enumerate(
            (
                (hs.at[0], hr.at[0], {"slab": up}),
                (hs.at[1], hr.at[1], {"slab": down}),
                (hsw.at[0], hrw.at[0], {"wheel": nxt}),
                (hsw.at[1], hrw.at[1], {"wheel": prv}),
            )
        )
    ]
    for copy in halos:
        copy.start()

    lane = lax.broadcasted_iota(jnp.int32, (32, 128), 1)
    spot = lane // 32

    def pack(t, res):
        for h in range(2):
            part = [res[:, c, :, h * 128 : (h + 1) * 128].reshape(32, 128) for c in range(3)]
            one = pltpu.roll(part[1], 32, 1)
            two = pltpu.roll(part[2], 64, 1)
            for g in range(4):
                tile = jnp.where(
                    spot == (g + 1) % 4, one, jnp.where(spot == (g + 2) % 4, two, part[0])
                )
                for half in range(2):
                    rows = jnp.concatenate(
                        (tile[half * 8 : half * 8 + 8], tile[16 + half * 8 : 24 + half * 8]), axis=0
                    )
                    sb[t, (h * 4 + g) * 2 + half] = rows.astype(BF)

    def send(t):
        @pl.loop(0, 16)
        def _(i):
            gv = lax.rem(w // 2 + i, 16)
            to = gv * 2 + t

            @pl.when(to != w)
            def _():
                pltpu.make_async_remote_copy(
                    src_ref=sb.at[t, gv], dst_ref=rv1.at[w], send_sem=ssem1, recv_sem=rsem1,
                    device_id={"wheel": to}, device_id_type=MESH,
                ).start()

    pack(0, v - shift_value * u)
    send(0)

    def stencil(ke, k, picked):
        picked = picked.reshape(2, 3, 16, 256)
        for c in range(3):
            for d in range(3):
                ke[c] = ke[c] + st[c, d, k : k + 1, :] * picked[:, d]
        return ke

    own = jnp.concatenate((ehi, elo), axis=0)
    ke = [jnp.zeros((2, 16, 256), F32) for _ in range(3)]
    for k in range(8):
        both = jnp.dot(own, one_hot(256, 256, nb[k : k + 1, :]), preferred_element_type=F32)
        ke = stencil(ke, k, both[:96] + both[96:])

    for copy in halos:
        copy.wait()
    zero = jnp.zeros((96, 128), F32)
    iface = jnp.where(j > 0, hr[0].astype(F32), zero) + jnp.where(j < SLAB - 1, hr[1].astype(F32), zero)
    face = jnp.concatenate(
        (
            hrw[0].astype(F32) + picks[48:96, 384:512],
            hrw[1].astype(F32) + picks[0:48, 256:384],
        ),
        axis=0,
    )
    halo = jnp.concatenate((iface, face), axis=1).astype(BF)
    for k in range(8):
        ke = stencil(
            ke, k, jnp.dot(halo, one_hot(256, 256, nb[k : k + 1, :] - 256), preferred_element_type=F32)
        )

    mass = [ms[c : c + 1, :] for c in range(3)]
    gyro = (-(mass[0] * v[:, 1]), mass[1] * v[:, 0], None)
    rows = []
    for c in range(3):
        scaled = jnp.stack(
            [(1.0 + class_step * bc[s].astype(F32)) * ke[c][s] for s in range(2)], axis=0
        )
        row = -scaled - shift_value * (mass[c] * v[:, c])
        if c < 2:
            row = row - gyro_rate * gyro[c]
        rows.append(row)
    pack(1, jnp.stack(rows, axis=1))
    send(1)

    rv1[w] = sb[lax.rem(w, 2), w // 2]
    pltpu.make_async_copy(rv1.at[pl.ds(0, WHEEL - 1)], rv1.at[pl.ds(0, WHEEL - 1)], rsem1).wait()
    copy_km.wait()
    field = rv1[...].reshape(512, 128)
    har = jnp.dot(kmv[0], field, preferred_element_type=F32) + jnp.dot(
        kmv[1], field, preferred_element_type=F32
    )
    sb2[...] = har.astype(BF).reshape(32, 16, 128)

    @pl.loop(1, WHEEL)
    def _(i):
        to = lax.rem(w + i, WHEEL)
        pltpu.make_async_remote_copy(
            src_ref=sb2.at[to], dst_ref=rv2.at[w], send_sem=ssem2, recv_sem=rsem2,
            device_id={"wheel": to}, device_id_type=MESH,
        ).start()

    rv2[w] = sb2[w]
    pltpu.make_async_copy(rv2.at[pl.ds(0, WHEEL - 1)], rv2.at[pl.ds(0, WHEEL - 1)], rsem2).wait()
    copy_pc.wait()
    lane16 = lax.broadcasted_iota(jnp.int32, (16, 128), 1)
    for g in range(8):
        turned = []
        for q in range(2):
            for t in range(2):
                x = jnp.concatenate(
                    [
                        rv2[(g * 2 + half) * 2 + t].astype(F32)[q * 8 : q * 8 + 8]
                        for half in range(2)
                    ],
                    axis=0,
                )
                shift = (96 * (2 * q + t) - 32 * (g % 4)) % 128
                turned.append(pltpu.roll(x, shift, 1) if shift else x)
        lhs = jnp.concatenate(
            (
                jnp.where(lane16 < 96, turned[0], turned[1]),
                jnp.where(lane16 < 64, turned[1], turned[2]),
                jnp.where(lane16 < 32, turned[2], turned[3]),
            ),
            axis=1,
        ).astype(BF)
        out[0, g] = lax.dot_general(
            lhs, pcv[0, g], (((1,), (1,)), ((), ())), preferred_element_type=F32
        )

    pltpu.make_async_copy(rv1.at[pl.ds(0, WHEEL - 1)], rv1.at[pl.ds(0, WHEEL - 1)], ssem1).wait()
    pltpu.make_async_copy(rv2.at[pl.ds(0, WHEEL - 1)], rv2.at[pl.ds(0, WHEEL - 1)], ssem2).wait()


def on_device(
    krylov_block, blade_class, neighbors, iface_rows, face_rows, stiffness, lumped_mass, precond
):
    vmem = pl.BlockSpec(memory_space=pltpu.VMEM)
    hbm = pl.BlockSpec(memory_space=pl.ANY)
    return pl.pallas_call(
        kernel,
        out_shape=jax.ShapeDtypeStruct((1, 8, 16, 384), F32),
        in_specs=[vmem, pl.BlockSpec(memory_space=pltpu.SMEM)] + [vmem] * 5 + [hbm, hbm],
        out_specs=vmem,
        scratch_shapes=[
            pltpu.VMEM((1, 8, 384, 384), BF),
            pltpu.VMEM((2, 512, 512), BF),
            pltpu.VMEM((2, 96, 128), BF),
            pltpu.VMEM((2, 48, 128), BF),
            pltpu.VMEM((2, 96, 128), BF),
            pltpu.VMEM((2, 48, 128), BF),
            pltpu.VMEM((2, 16, 16, 128), BF),
            pltpu.VMEM((32, 16, 128), BF),
            pltpu.VMEM((32, 16, 128), BF),
            pltpu.VMEM((32, 16, 128), BF),
            pltpu.SemaphoreType.DMA((2,)),
            pltpu.SemaphoreType.DMA((4,)),
            pltpu.SemaphoreType.DMA((4,)),
            pltpu.SemaphoreType.DMA,
            pltpu.SemaphoreType.DMA,
            pltpu.SemaphoreType.DMA,
            pltpu.SemaphoreType.DMA,
        ],
        compiler_params=pltpu.CompilerParams(
            collective_id=0, has_side_effects=True, vmem_limit_bytes=40 * 1024 * 1024
        ),
    )(
        krylov_block, blade_class, neighbors, iface_rows, face_rows, stiffness, lumped_mass,
        precond, jnp.asarray(kron_table()),
    )


def solution(mesh):
    return jax.shard_map(
        on_device,
        mesh=mesh,
        in_specs=(
            P(None, "wheel", None, None, "slab"),
            P("wheel"),
            P(None, "slab"),
            P(None, "slab"),
            P(None, "slab"),
            P(None, None, None, "slab"),
            P(None, "slab"),
            P("wheel", "slab", None, None),
        ),
        out_specs=P("wheel", "slab", None, None),
        check_vma=False,
    )
```

time: 239 us -> 39.6 us (0.17); the launches traced: 235 us -> 39.3 us
  waiting for transfers between devices: 138 us -> 0 us
  local copies, waits for them, and re-layouts: 41.8 us -> 8.77 us
  Pallas kernels: 0 us -> 30.5 us
  matrix products: 18.5 us -> 0 us
  other arithmetic: 13.8 us -> 0 us
  between operations: 13.6 us -> 0.02 us
  starting transfers between devices: 9.77 us -> 0 us
    reduce_scatter x1 -> x0, waiting for transfers between devices: 138 us -> none  [on_device(): lax.psum_scatter(jnp.einsum('bs,tscvn->btcvn', table, residual, precision...]
    pallas_call x0 -> x1, Pallas kernels: none -> 30.5 us  [on_device(): pl.pallas_call(kernel, out_shape=jax.ShapeDtypeStruct((1, 8, 16, 384), F3...]
    gather x9 -> x0, local copies, waits for them, and re-layouts: 28.5 us -> none  [the longest x1 23.2 us: on_device(): picked = jnp.take(extended, neighbors, axis=3)]
    dot_general x3 -> x0, matrix products: 18.5 us -> none  [the longest x1 10.7 us: on_device(): jnp.einsum('cdkn,sdvkn->scvn', stiffness, picked, precision=lax.Precision...]
    ppermute x4 -> x0, starting transfers between devices: 9.77 us -> none  [the longest x2 5.27 us: extended_2(): lax.ppermute(lax.slice_in_dim(block, block.shape[dim] - width, None, axis...]
    dot_general x2 -> x0, local copies, waits for them, and re-layouts: 6.69 us -> none  [the longest x1 6.31 us: on_device(): jnp.einsum('bs,tscvn->btcvn', table, residual, precision=lax.Precision.HI...]
    unnamed x4 -> x19, local copies, waits for them, and re-layouts: 2.22 us -> 8.77 us
  transfers between devices with their start and end apart: 5 -> 0, of which waited for: 1 -> 0; matrix products, arithmetic and copies ran while one was open for 7% -> 0% of each run, Pallas kernels for 0% -> 0%
where the time goes in v1:
time: 39.6 us; the launch traced here: 39.3 us
  Pallas kernels  30.5 us (77%)
  local copies, waits for them, and re-layouts  8.77 us (22%)
    pallas_call x1, Pallas kernels, on_device(): pl.pallas_call(kernel, out_shape=jax.ShapeDtypeStruct((1, 8, 16, 384), F3...  30.5 us
    unnamed x19, local copies, waits for them, and re-layouts  8.77 us

profile of v1, /device:TPU:1, one launch (start us, length us, event | category | flops | bytes accessed | tf_op | source)
XLA Modules:
  0.0 39.3 jit_solution(17041319619060522455)
XLA Ops:
  0.0 0.0 copy-start
  0.0 1.7 %copy-done = bf16[1,8,384,384]{3,2,1,0:T(8,128)(2,1)S(1)} copy-done((bf16[1,8,384,384]{3,2,1,0:T(8,128)(2,1)S(1)}, bf16[1,8,384,384]{3,2,1,0:T(8,128)(2,1)}, u32[]{:S(2)}) %copy-start) | copy-done | bytes 2359320
  1.7 0.0 copy-start.1
  1.7 1.2 %copy-done.1 = bf16[2,512,512]{2,1,0:T(8,128)(2,1)S(1)} copy-done((bf16[2,512,512]{2,1,0:T(8,128)(2,1)S(1)}, bf16[2,512,512]{2,1,0:T(8,128)(2,1)}, u32[]{:S(2)}) %copy-start.1) | copy-done | bytes 1048600
  2.9 0.0 copy-start.2
  2.9 0.9 %copy-done.2 = f32[2,2,3,16,256]{4,3,2,1,0:T(8,128)S(1)} copy-done((f32[2,2,3,16,256]{4,3,2,1,0:T(8,128)S(1)}, f32[2,2,3,16,256]{4,3,2,1,0:T(8,128)}, u32[]{:S(2)}) %copy-start.2) | copy-done | bytes 196632
  3.8 0.0 copy-start.3
  3.8 0.9 %copy-done.3 = f32[3,3,8,256]{3,2,1,0:T(8,128)S(1)} copy-done((f32[3,3,8,256]{3,2,1,0:T(8,128)S(1)}, f32[3,3,8,256]{3,2,1,0:T(8,128)}, u32[]{:S(2)}) %copy-start.3) | copy-done | bytes 73752
  4.7 0.0 copy-start.4
  4.7 0.7 %copy-done.4 = s32[8,256]{1,0:T(8,128)S(1)} copy-done((s32[8,256]{1,0:T(8,128)S(1)}, s32[8,256]{1,0:T(8,128)}, u32[]{:S(2)}) %copy-start.4) | copy-done | bytes 8216
  5.4 0.0 copy-start.5
  5.4 0.7 %copy-done.5 = f32[3,256]{1,0:T(4,128)S(1)} copy-done((f32[3,256]{1,0:T(4,128)S(1)}, f32[3,256]{1,0:T(4,128)}, u32[]{:S(2)}) %copy-start.5) | copy-done | bytes 3096
  6.1 0.0 copy-start.6
  6.1 0.7 %copy-done.6 = s32[2,64]{1,0:T(2,128)S(1)} copy-done((s32[2,64]{1,0:T(2,128)S(1)}, s32[2,64]{1,0:T(2,128)}, u32[]{:S(2)}) %copy-start.6) | copy-done | bytes 536
  6.8 0.0 copy-start.7
  6.8 0.7 %copy-done.7 = s32[2,64]{1,0:T(2,128)S(1)} copy-done((s32[2,64]{1,0:T(2,128)S(1)}, s32[2,64]{1,0:T(2,128)}, u32[]{:S(2)}) %copy-start.7) | copy-done | bytes 536
  7.4 0.0 copy-start.8
  7.4 0.7 %copy-done.8 = s32[2]{0:T(128)S(1)} copy-done((s32[2]{0:T(128)S(1)}, s32[2]{0:T(128)}, u32[]{:S(2)}) %copy-start.8) | copy-done | bytes 32
  8.1 30.5 %shard_map.91 = f32[1,8,16,384]{3,2,1,0:T(8,128)S(1)} custom-call(f32[2,2,3,16,256]{4,3,2,1,0:T(8,128)S(1)} %copy-done.2, s32[2]{0:T(128)S(1)} %copy-done.8, s32[8,256]{1,0:T(8,128)S(1)} %copy-done.4, s32[2,64]{1,0:T(2,128)S(1)} %copy-done.6, s32[2,64]{1,0:T(2,128)S(1)} %copy-done.7, f32[3,3,8,256]{3,2,1,0:T(8,128)S(1)} %copy-done.3, ...), custom_call_target="tpu_custom_call" | custom-call | tf_op jit(solution)/shard_map/pallas_call | solution.py:244
  38.6 0.7 %copy.11 = f32[1,8,16,384]{3,2,1,0:T(8,128)} copy(f32[1,8,16,384]{3,2,1,0:T(8,128)S(1)} %shard_map.91) | data formatting | bytes 393216
Async XLA Ops:
  0.0 1.7 %copy-start = (bf16[1,8,384,384]{3,2,1,0:T(8,128)(2,1)S(1)}, bf16[1,8,384,384]{3,2,1,0:T(8,128)(2,1)}, u32[]{:S(2)}) copy-start(bf16[1,8,384,384]{3,2,1,0:T(8,128)(2,1)} %pc_hbm.1) | copy-start | bytes 7077892
  1.7 1.2 %copy-start.1 = (bf16[2,512,512]{2,1,0:T(8,128)(2,1)S(1)}, bf16[2,512,512]{2,1,0:T(8,128)(2,1)}, u32[]{:S(2)}) copy-start(bf16[2,512,512]{2,1,0:T(8,128)(2,1)} %constant.2.clone.km_hbm) | copy-start | bytes 3145732
  2.9 0.9 %copy-start.2 = (f32[2,2,3,16,256]{4,3,2,1,0:T(8,128)S(1)}, f32[2,2,3,16,256]{4,3,2,1,0:T(8,128)}, u32[]{:S(2)}) copy-start(f32[2,2,3,16,256]{4,3,2,1,0:T(8,128)} %kb.1) | copy-start | bytes 589828
  3.8 0.9 %copy-start.3 = (f32[3,3,8,256]{3,2,1,0:T(8,128)S(1)}, f32[3,3,8,256]{3,2,1,0:T(8,128)}, u32[]{:S(2)}) copy-start(f32[3,3,8,256]{3,2,1,0:T(8,128)} %st.1) | copy-start | bytes 221188
  4.7 0.7 %copy-start.4 = (s32[8,256]{1,0:T(8,128)S(1)}, s32[8,256]{1,0:T(8,128)}, u32[]{:S(2)}) copy-start(s32[8,256]{1,0:T(8,128)} %nb.1) | copy-start | bytes 24580
  5.4 0.7 %copy-start.5 = (f32[3,256]{1,0:T(4,128)S(1)}, f32[3,256]{1,0:T(4,128)}, u32[]{:S(2)}) copy-start(f32[3,256]{1,0:T(4,128)} %ms.1) | copy-start | bytes 9220
  6.1 0.7 %copy-start.6 = (s32[2,64]{1,0:T(2,128)S(1)}, s32[2,64]{1,0:T(2,128)}, u32[]{:S(2)}) copy-start(s32[2,64]{1,0:T(2,128)} %ifr.1) | copy-start | bytes 1540
  6.8 0.7 %copy-start.7 = (s32[2,64]{1,0:T(2,128)S(1)}, s32[2,64]{1,0:T(2,128)}, u32[]{:S(2)}) copy-start(s32[2,64]{1,0:T(2,128)} %fcr.1) | copy-start | bytes 1540
  7.4 0.7 %copy-start.8 = (s32[2]{0:T(128)S(1)}, s32[2]{0:T(128)}, u32[]{:S(2)}) copy-start(s32[2]{0:T(128)} %bc.1) | copy-start | bytes 28

commit v2 on v1

--- a/solution.py
+++ b/solution.py
@@ -46,12 +46,24 @@
 
 
 def kernel(
-    kb, bc, nb, ifr, fcr, st, ms, pc_hbm, km_hbm, out,
-    pcv, kmv, hs, hsw, hr, hrw, sb, rv1, sb2, rv2,
+    kb_hbm, bc_hbm, nb_hbm, ifr_hbm, fcr_hbm, st_hbm, ms_hbm, pc_hbm, km_hbm, out,
+    kb, bc, nb, ifr, fcr, st, ms, pcv, kmv, hs, hsw, hr, hrw, sb, rv1, sb2, rv2,
     lsem, hsend, hrecv, ssem1, rsem1, ssem2, rsem2,
 ):
     w = lax.axis_index("wheel")
     j = lax.axis_index("slab")
+
+    loads = [
+        pltpu.make_async_copy(src, dst, lsem.at[n])
+        for n, (src, dst) in enumerate(
+            (
+                (kb_hbm, kb), (ifr_hbm, ifr), (fcr_hbm, fcr), (nb_hbm, nb), (st_hbm, st),
+                (ms_hbm, ms), (bc_hbm, bc), (km_hbm, kmv), (pc_hbm, pcv),
+            )
+        )
+    ]
+    for load in loads:
+        load.start()
 
     barrier = pltpu.get_barrier_semaphore()
 
@@ -68,11 +80,8 @@
     for slab in (up, down):
         pl.semaphore_signal(barrier, inc=1, device_id={"slab": slab}, device_id_type=MESH)
 
-    copy_km = pltpu.make_async_copy(km_hbm, kmv, lsem.at[0])
-    copy_pc = pltpu.make_async_copy(pc_hbm, pcv, lsem.at[1])
-    copy_km.start()
-    copy_pc.start()
-
+    for load in loads[:3]:
+        load.wait()
     u = kb[0]
     v = kb[1]
     e = (u + damping_ratio * v).reshape(96, 256)
@@ -149,6 +158,8 @@
                 ke[c] = ke[c] + st[c, d, k : k + 1, :] * picked[:, d]
         return ke
 
+    for load in loads[3:7]:
+        load.wait()
     own = jnp.concatenate((ehi, elo), axis=0)
     ke = [jnp.zeros((2, 16, 256), F32) for _ in range(3)]
     for k in range(8):
@@ -188,7 +199,7 @@
 
     rv1[w] = sb[lax.rem(w, 2), w // 2]
     pltpu.make_async_copy(rv1.at[pl.ds(0, WHEEL - 1)], rv1.at[pl.ds(0, WHEEL - 1)], rsem1).wait()
-    copy_km.wait()
+    loads[7].wait()
     field = rv1[...].reshape(512, 128)
     har = jnp.dot(kmv[0], field, preferred_element_type=F32) + jnp.dot(
         kmv[1], field, preferred_element_type=F32
@@ -205,7 +216,7 @@
 
     rv2[w] = sb2[w]
     pltpu.make_async_copy(rv2.at[pl.ds(0, WHEEL - 1)], rv2.at[pl.ds(0, WHEEL - 1)], rsem2).wait()
-    copy_pc.wait()
+    loads[8].wait()
     lane16 = lax.broadcasted_iota(jnp.int32, (16, 128), 1)
     for g in range(8):
         turned = []
@@ -240,13 +251,20 @@
     krylov_block, blade_class, neighbors, iface_rows, face_rows, stiffness, lumped_mass, precond
 ):
     vmem = pl.BlockSpec(memory_space=pltpu.VMEM)
-    hbm = pl.BlockSpec(memory_space=pl.ANY)
+    hbm = pl.BlockSpec(memory_space=pltpu.HBM)
     return pl.pallas_call(
         kernel,
         out_shape=jax.ShapeDtypeStruct((1, 8, 16, 384), F32),
-        in_specs=[vmem, pl.BlockSpec(memory_space=pltpu.SMEM)] + [vmem] * 5 + [hbm, hbm],
+        in_specs=[hbm] * 9,
         out_specs=vmem,
         scratch_shapes=[
+            pltpu.VMEM((2, 2, 3, 16, 256), F32),
+            pltpu.SMEM((2,), jnp.int32),
+            pltpu.VMEM((8, 256), jnp.int32),
+            pltpu.VMEM((2, 64), jnp.int32),
+            pltpu.VMEM((2, 64), jnp.int32),
+            pltpu.VMEM((3, 3, 8, 256), F32),
+            pltpu.VMEM((3, 256), F32),
             pltpu.VMEM((1, 8, 384, 384), BF),
             pltpu.VMEM((2, 512, 512), BF),
             pltpu.VMEM((2, 96, 128), BF),
@@ -257,7 +275,7 @@
             pltpu.VMEM((32, 16, 128), BF),
             pltpu.VMEM((32, 16, 128), BF),
             pltpu.VMEM((32, 16, 128), BF),
-            pltpu.SemaphoreType.DMA((2,)),
+            pltpu.SemaphoreType.DMA((9,)),
             pltpu.SemaphoreType.DMA((4,)),
             pltpu.SemaphoreType.DMA((4,)),
             pltpu.SemaphoreType.DMA,
@@ -266,7 +284,7 @@
             pltpu.SemaphoreType.DMA,
         ],
         compiler_params=pltpu.CompilerParams(
-            collective_id=0, has_side_effects=True, vmem_limit_bytes=40 * 1024 * 1024
+            collective_id=0, has_side_effects=True, vmem_limit_bytes=60 * 1024 * 1024
         ),
     )(
         krylov_block, blade_class, neighbors, iface_rows, face_rows, stiffness, lumped_mass,

time: 39.6 us -> 32.4 us (0.82)
  local copies, waits for them, and re-layouts: 8.77 us -> 1.62 us
    unnamed x19 -> x1, local copies, waits for them, and re-layouts: 8.77 us -> 1.62 us
where the time goes in v2:
time: 32.4 us; the launch traced here: 32.3 us
  Pallas kernels  30.7 us (95%)
  local copies, waits for them, and re-layouts  1.62 us (5%)
    pallas_call x1, Pallas kernels, on_device(): pl.pallas_call(kernel, out_shape=jax.ShapeDtypeStruct((1, 8, 16, 384), F3...  30.7 us
    unnamed x1, local copies, waits for them, and re-layouts  1.62 us

profile of v2, /device:TPU:1, one launch (start us, length us, event | category | flops | bytes accessed | tf_op | source)
XLA Modules:
  0.0 32.3 jit_solution(739179618782985799)
XLA Ops:
  0.0 30.7 %shard_map.91 = f32[1,8,16,384]{3,2,1,0:T(8,128)} custom-call(f32[2,2,3,16,256]{4,3,2,1,0:T(8,128)} %kb_hbm.1, s32[2]{0:T(128)} %bc_hbm.1, s32[8,256]{1,0:T(8,128)} %nb_hbm.1, s32[2,64]{1,0:T(2,128)} %ifr_hbm.1, s32[2,64]{1,0:T(2,128)} %fcr_hbm.1, f32[3,3,8,256]{3,2,1,0:T(8,128)} %st_hbm.1, f32[3,256]{1,0:T(4,128)} %ms_hbm.1, ...), custom_call_target="tpu_custom_call" | custom-call | tf_op jit(solution)/shard_map/pallas_call | solution.py:255
  30.7 1.6 %copy.11 = f32[1,8,16,384]{3,2,1,0:T(8,128)} copy(f32[1,8,16,384]{3,2,1,0:T(8,128)} %shard_map.91) | data formatting | bytes 393216

commit v3 on v2

--- a/solution.py
+++ b/solution.py
@@ -21,6 +21,14 @@
 MESH = pl.DeviceIdType.MESH
 BF = jnp.bfloat16
 F32 = jnp.float32
+
+
+def slot_of(w):
+    return (w // 8 % 2) * 16 + (w // 16) * 8 + w % 8
+
+
+def worker_of(t, g):
+    return (12 + g) % 16 if t else 16 + g
 
 
 def basis_table():
@@ -34,7 +42,8 @@
 
 
 def kron_table():
-    full = np.kron(basis_table(), np.eye(8, dtype=np.float32))
+    sectors = [2 * w + part for w in sorted(range(WHEEL), key=slot_of) for part in range(2)]
+    full = np.kron(basis_table()[:, sectors], np.eye(8, dtype=np.float32))
     high = full.astype(ml_dtypes.bfloat16)
     low = (full - high.astype(np.float32)).astype(ml_dtypes.bfloat16)
     return np.stack((high, low))
@@ -47,7 +56,7 @@
 
 def kernel(
     kb_hbm, bc_hbm, nb_hbm, ifr_hbm, fcr_hbm, st_hbm, ms_hbm, pc_hbm, km_hbm, out,
-    kb, bc, nb, ifr, fcr, st, ms, pcv, kmv, hs, hsw, hr, hrw, sb, rv1, sb2, rv2,
+    kb, bc, nb, ifr, fcr, st, ms, pcv, kmv, hs, hsw, hr, hrw, sb, rv1, acc, sb2, rv2,
     lsem, hsend, hrecv, ssem1, rsem1, ssem2, rsem2,
 ):
     w = lax.axis_index("wheel")
@@ -67,18 +76,24 @@
 
     barrier = pltpu.get_barrier_semaphore()
 
-    @pl.loop(1, WHEEL)
-    def _(i):
-        pl.semaphore_signal(
-            barrier, inc=1, device_id={"wheel": lax.rem(w + i, WHEEL)}, device_id_type=MESH
-        )
-
     up = lax.rem(j + 1, SLAB)
     down = lax.rem(j + SLAB - 1, SLAB)
     nxt = lax.rem(w + 1, WHEEL)
     prv = lax.rem(w + WHEEL - 1, WHEEL)
-    for slab in (up, down):
-        pl.semaphore_signal(barrier, inc=1, device_id={"slab": slab}, device_id_type=MESH)
+    for to in ({"wheel": nxt}, {"wheel": prv}, {"slab": up}, {"slab": down}):
+        pl.semaphore_signal(barrier, inc=1, device_id=to, device_id_type=MESH)
+
+    my_t = jnp.where(w < 16, 1, 0)
+    my_g = jnp.where(w < 16, lax.rem(w + 4, 16), w - 16)
+    works = my_g < 8
+
+    @pl.when(works)
+    def _():
+        @pl.loop(1, WHEEL)
+        def _(i):
+            pl.semaphore_signal(
+                barrier, inc=1, device_id={"wheel": lax.rem(w + i, WHEEL)}, device_id_type=MESH
+            )
 
     for load in loads[:3]:
         load.wait()
@@ -98,7 +113,7 @@
     hsw[0] = picks[48:96, 256:384].astype(BF)
     hsw[1] = picks[0:48, 384:512].astype(BF)
 
-    pl.semaphore_wait(barrier, WHEEL + 1)
+    pl.semaphore_wait(barrier, jnp.where(works, 19, 20))
 
     halos = [
         pltpu.make_async_remote_copy(
@@ -133,20 +148,25 @@
                     rows = jnp.concatenate(
                         (tile[half * 8 : half * 8 + 8], tile[16 + half * 8 : 24 + half * 8]), axis=0
                     )
-                    sb[t, (h * 4 + g) * 2 + half] = rows.astype(BF)
+                    sb[t, h * 4 + g, half] = rows.astype(BF)
+
+    slot = lax.rem(w // 8, 2) * 16 + (w // 16) * 8 + lax.rem(w, 8)
+    half_sem = rsem1.at[lax.rem(w // 8, 2)]
 
     def send(t):
-        @pl.loop(0, 16)
-        def _(i):
-            gv = lax.rem(w // 2 + i, 16)
-            to = gv * 2 + t
-
-            @pl.when(to != w)
+        for g in range(8):
+            to = worker_of(t, g)
+
+            @pl.when(w != to)
             def _():
                 pltpu.make_async_remote_copy(
-                    src_ref=sb.at[t, gv], dst_ref=rv1.at[w], send_sem=ssem1, recv_sem=rsem1,
+                    src_ref=sb.at[t, g], dst_ref=rv1.at[slot], send_sem=ssem1, recv_sem=half_sem,
                     device_id={"wheel": to}, device_id_type=MESH,
                 ).start()
+
+            @pl.when(w == to)
+            def _():
+                pltpu.make_async_copy(sb.at[t, g], rv1.at[slot], half_sem).start()
 
     pack(0, v - shift_value * u)
     send(0)
@@ -197,38 +217,64 @@
     pack(1, jnp.stack(rows, axis=1))
     send(1)
 
-    rv1[w] = sb[lax.rem(w, 2), w // 2]
-    pltpu.make_async_copy(rv1.at[pl.ds(0, WHEEL - 1)], rv1.at[pl.ds(0, WHEEL - 1)], rsem1).wait()
-    loads[7].wait()
-    field = rv1[...].reshape(512, 128)
-    har = jnp.dot(kmv[0], field, preferred_element_type=F32) + jnp.dot(
-        kmv[1], field, preferred_element_type=F32
-    )
-    sb2[...] = har.astype(BF).reshape(32, 16, 128)
-
-    @pl.loop(1, WHEEL)
-    def _(i):
-        to = lax.rem(w + i, WHEEL)
-        pltpu.make_async_remote_copy(
-            src_ref=sb2.at[to], dst_ref=rv2.at[w], send_sem=ssem2, recv_sem=rsem2,
-            device_id={"wheel": to}, device_id_type=MESH,
-        ).start()
-
-    rv2[w] = sb2[w]
-    pltpu.make_async_copy(rv2.at[pl.ds(0, WHEEL - 1)], rv2.at[pl.ds(0, WHEEL - 1)], rsem2).wait()
+    @pl.when(works)
+    def _():
+        loads[7].wait()
+
+        def field(part):
+            both = rv1[part * 16 : part * 16 + 16]
+            return jnp.concatenate(
+                (both[:, 0].reshape(256, 128), both[:, 1].reshape(256, 128)), axis=1
+            )
+
+        def transform(first, part, data):
+            rows = slice(first * 256, first * 256 + 256)
+            cols = slice(part * 256, part * 256 + 256)
+            return jnp.dot(kmv[0, rows, cols], data, preferred_element_type=F32) + jnp.dot(
+                kmv[1, rows, cols], data, preferred_element_type=F32
+            )
+
+        def arrived(part):
+            whole = rv1.at[pl.ds(part * 16, 16)]
+            pltpu.make_async_copy(whole, whole, rsem1.at[part]).wait()
+
+        arrived(0)
+        near = field(0)
+        for first in range(2):
+            acc[first] = transform(first, 0, near)
+        arrived(1)
+        far = field(1)
+        for first in range(2):
+            har = (acc[first] + transform(first, 1, far)).reshape(16, 2, 8, 256)
+            sb2[first * 16 : first * 16 + 16] = jnp.concatenate(
+                (har[..., :128], har[..., 128:]), axis=2
+            ).astype(BF)
+            for z in (0, 1, 2, 3, 7, 6, 5, 4):
+                for core in range(2):
+                    to = first * 16 + z * 2 + core
+
+                    @pl.when(w != to)
+                    def _():
+                        pltpu.make_async_remote_copy(
+                            src_ref=sb2.at[to], dst_ref=rv2.at[my_t, my_g], send_sem=ssem2,
+                            recv_sem=rsem2.at[my_t], device_id={"wheel": to}, device_id_type=MESH,
+                        ).start()
+
+                    @pl.when(w == to)
+                    def _():
+                        pltpu.make_async_copy(
+                            sb2.at[to], rv2.at[my_t, my_g], rsem2.at[my_t]
+                        ).start()
+
+    for t in range(2):
+        pltpu.make_async_copy(rv2.at[t], rv2.at[t], rsem2.at[t]).wait()
     loads[8].wait()
     lane16 = lax.broadcasted_iota(jnp.int32, (16, 128), 1)
     for g in range(8):
         turned = []
         for q in range(2):
             for t in range(2):
-                x = jnp.concatenate(
-                    [
-                        rv2[(g * 2 + half) * 2 + t].astype(F32)[q * 8 : q * 8 + 8]
-                        for half in range(2)
-                    ],
-                    axis=0,
-                )
+                x = rv2[t, g, q].astype(F32)
                 shift = (96 * (2 * q + t) - 32 * (g % 4)) % 128
                 turned.append(pltpu.roll(x, shift, 1) if shift else x)
         lhs = jnp.concatenate(
@@ -243,8 +289,19 @@
             lhs, pcv[0, g], (((1,), (1,)), ((), ())), preferred_element_type=F32
         )
 
-    pltpu.make_async_copy(rv1.at[pl.ds(0, WHEEL - 1)], rv1.at[pl.ds(0, WHEEL - 1)], ssem1).wait()
-    pltpu.make_async_copy(rv2.at[pl.ds(0, WHEEL - 1)], rv2.at[pl.ds(0, WHEEL - 1)], ssem2).wait()
+    def sent(count, sem):
+        whole = rv1.at[pl.ds(0, count)]
+        pltpu.make_async_copy(whole, whole, sem).wait()
+
+    @pl.when(works)
+    def _():
+        sent(15, ssem1)
+        sent(31, ssem2)
+
+    @pl.when(jnp.logical_not(works))
+    def _():
+        loads[7].wait()
+        sent(16, ssem1)
 
 
 def on_device(
@@ -271,17 +328,18 @@
             pltpu.VMEM((2, 48, 128), BF),
             pltpu.VMEM((2, 96, 128), BF),
             pltpu.VMEM((2, 48, 128), BF),
-            pltpu.VMEM((2, 16, 16, 128), BF),
-            pltpu.VMEM((32, 16, 128), BF),
-            pltpu.VMEM((32, 16, 128), BF),
-            pltpu.VMEM((32, 16, 128), BF),
+            pltpu.VMEM((2, 8, 2, 16, 128), BF),
+            pltpu.VMEM((32, 2, 16, 128), BF),
+            pltpu.VMEM((2, 256, 256), F32),
+            pltpu.VMEM((32, 2, 16, 128), BF),
+            pltpu.VMEM((2, 8, 2, 16, 128), BF),
             pltpu.SemaphoreType.DMA((9,)),
             pltpu.SemaphoreType.DMA((4,)),
             pltpu.SemaphoreType.DMA((4,)),
             pltpu.SemaphoreType.DMA,
+            pltpu.SemaphoreType.DMA((2,)),
             pltpu.SemaphoreType.DMA,
-            pltpu.SemaphoreType.DMA,
-            pltpu.SemaphoreType.DMA,
+            pltpu.SemaphoreType.DMA((2,)),
         ],
         compiler_params=pltpu.CompilerParams(
             collective_id=0, has_side_effects=True, vmem_limit_bytes=60 * 1024 * 1024

time: 32.4 us -> 32.8 us (1.012)
  Pallas kernels: 30.7 us -> 31.1 us
    pallas_call x1, Pallas kernels: 30.7 us -> 31.1 us  [on_device(): pl.pallas_call(kernel, out_shape=jax.ShapeDtypeStruct((1, 8, 16, 384), F3...]
where the time goes in v3:
time: 32.8 us; the launch traced here: 32.7 us
  Pallas kernels  31.1 us (95%)
  local copies, waits for them, and re-layouts  1.62 us (5%)
    pallas_call x1, Pallas kernels, on_device(): pl.pallas_call(kernel, out_shape=jax.ShapeDtypeStruct((1, 8, 16, 384), F3...  31.1 us
    unnamed x1, local copies, waits for them, and re-layouts  1.62 us

profile of v3, /device:TPU:1, one launch (start us, length us, event | category | flops | bytes accessed | tf_op | source)
XLA Modules:
  0.0 32.7 jit_solution(3504804629156671703)
XLA Ops:
  0.0 31.1 %shard_map.91 = f32[1,8,16,384]{3,2,1,0:T(8,128)} custom-call(f32[2,2,3,16,256]{4,3,2,1,0:T(8,128)} %kb_hbm.1, s32[2]{0:T(128)} %bc_hbm.1, s32[8,256]{1,0:T(8,128)} %nb_hbm.1, s32[2,64]{1,0:T(2,128)} %ifr_hbm.1, s32[2,64]{1,0:T(2,128)} %fcr_hbm.1, f32[3,3,8,256]{3,2,1,0:T(8,128)} %st_hbm.1, f32[3,256]{1,0:T(4,128)} %ms_hbm.1, ...), custom_call_target="tpu_custom_call" | custom-call | tf_op jit(solution)/shard_map/pallas_call | solution.py:312
  31.1 1.6 %copy.11 = f32[1,8,16,384]{3,2,1,0:T(8,128)} copy(f32[1,8,16,384]{3,2,1,0:T(8,128)} %shard_map.91) | data formatting | bytes 393216

commit v4 on v3

--- a/solution.py
+++ b/solution.py
@@ -28,7 +28,7 @@
 
 
 def worker_of(t, g):
-    return (12 + g) % 16 if t else 16 + g
+    return (g // 4) * 16 + ((7 + g % 4) % 8) * 2 + t
 
 
 def basis_table():
@@ -62,6 +62,10 @@
     w = lax.axis_index("wheel")
     j = lax.axis_index("slab")
 
+    up = lax.rem(j + 1, SLAB)
+    down = lax.rem(j + SLAB - 1, SLAB)
+    nxt = lax.rem(w + 1, WHEEL)
+    prv = lax.rem(w + WHEEL - 1, WHEEL)
     loads = [
         pltpu.make_async_copy(src, dst, lsem.at[n])
         for n, (src, dst) in enumerate(
@@ -75,25 +79,33 @@
         load.start()
 
     barrier = pltpu.get_barrier_semaphore()
-
-    up = lax.rem(j + 1, SLAB)
-    down = lax.rem(j + SLAB - 1, SLAB)
-    nxt = lax.rem(w + 1, WHEEL)
-    prv = lax.rem(w + WHEEL - 1, WHEEL)
-    for to in ({"wheel": nxt}, {"wheel": prv}, {"slab": up}, {"slab": down}):
+    has_up = j < SLAB - 1
+    has_down = j > 0
+
+    def greet(to):
         pl.semaphore_signal(barrier, inc=1, device_id=to, device_id_type=MESH)
 
-    my_t = jnp.where(w < 16, 1, 0)
-    my_g = jnp.where(w < 16, lax.rem(w + 4, 16), w - 16)
-    works = my_g < 8
+    @pl.when(has_up)
+    def _():
+        greet({"slab": up})
+
+    @pl.when(has_down)
+    def _():
+        greet({"slab": down})
+
+    greet({"wheel": nxt})
+    greet({"wheel": prv})
+
+    my_t = lax.rem(w, 2)
+    along = lax.rem(lax.rem(w // 2, 8) + 1, 8)
+    my_g = (w // 16) * 4 + along
+    works = along < 4
 
     @pl.when(works)
     def _():
         @pl.loop(1, WHEEL)
         def _(i):
-            pl.semaphore_signal(
-                barrier, inc=1, device_id={"wheel": lax.rem(w + i, WHEEL)}, device_id_type=MESH
-            )
+            greet({"wheel": lax.rem(w + i, WHEEL)})
 
     for load in loads[:3]:
         load.wait()
@@ -113,7 +125,10 @@
     hsw[0] = picks[48:96, 256:384].astype(BF)
     hsw[1] = picks[0:48, 384:512].astype(BF)
 
-    pl.semaphore_wait(barrier, jnp.where(works, 19, 20))
+    pl.semaphore_wait(
+        barrier,
+        18 + jnp.where(has_up, 1, 0) + jnp.where(has_down, 1, 0) - jnp.where(works, 1, 0),
+    )
 
     halos = [
         pltpu.make_async_remote_copy(
@@ -129,8 +144,17 @@
             )
         )
     ]
-    for copy in halos:
-        copy.start()
+
+    @pl.when(has_up)
+    def _():
+        halos[0].start()
+
+    @pl.when(has_down)
+    def _():
+        halos[1].start()
+
+    halos[2].start()
+    halos[3].start()
 
     lane = lax.broadcasted_iota(jnp.int32, (32, 128), 1)
     spot = lane // 32
@@ -186,10 +210,27 @@
         both = jnp.dot(own, one_hot(256, 256, nb[k : k + 1, :]), preferred_element_type=F32)
         ke = stencil(ke, k, both[:96] + both[96:])
 
-    for copy in halos:
-        copy.wait()
-    zero = jnp.zeros((96, 128), F32)
-    iface = jnp.where(j > 0, hr[0].astype(F32), zero) + jnp.where(j < SLAB - 1, hr[1].astype(F32), zero)
+    @pl.when(has_up)
+    def _():
+        halos[0].wait_send()
+        halos[1].wait_recv()
+
+    @pl.when(jnp.logical_not(has_up))
+    def _():
+        hr[1] = jnp.zeros((96, 128), BF)
+
+    @pl.when(has_down)
+    def _():
+        halos[1].wait_send()
+        halos[0].wait_recv()
+
+    @pl.when(jnp.logical_not(has_down))
+    def _():
+        hr[0] = jnp.zeros((96, 128), BF)
+
+    halos[2].wait()
+    halos[3].wait()
+    iface = hr[0].astype(F32) + hr[1].astype(F32)
     face = jnp.concatenate(
         (
             hrw[0].astype(F32) + picks[48:96, 384:512],
@@ -217,6 +258,10 @@
     pack(1, jnp.stack(rows, axis=1))
     send(1)
 
+    def sent(count, sem):
+        whole = rv1.at[pl.ds(0, count)]
+        pltpu.make_async_copy(whole, whole, sem).wait()
+
     @pl.when(works)
     def _():
         loads[7].wait()
@@ -237,6 +282,29 @@
         def arrived(part):
             whole = rv1.at[pl.ds(part * 16, 16)]
             pltpu.make_async_copy(whole, whole, rsem1.at[part]).wait()
+
+        def answer(to, group):
+            @pl.when(w != to)
+            def _():
+                pltpu.make_async_remote_copy(
+                    src_ref=sb2.at[to], dst_ref=rv2.at[my_t, my_g], send_sem=ssem2.at[group],
+                    recv_sem=rsem2.at[my_t], device_id={"wheel": to}, device_id_type=MESH,
+                ).start()
+
+            @pl.when(w == to)
+            def _():
+                pltpu.make_async_copy(sb2.at[to], rv2.at[my_t, my_g], rsem2.at[my_t]).start()
+
+        def left(group):
+            mine = lax.rem(w // 8, 2) == group
+
+            @pl.when(mine)
+            def _():
+                sent(15, ssem2.at[group])
+
+            @pl.when(jnp.logical_not(mine))
+            def _():
+                sent(16, ssem2.at[group])
 
         arrived(0)
         near = field(0)
@@ -249,22 +317,15 @@
             sb2[first * 16 : first * 16 + 16] = jnp.concatenate(
                 (har[..., :128], har[..., 128:]), axis=2
             ).astype(BF)
-            for z in (0, 1, 2, 3, 7, 6, 5, 4):
+            for z in range(4):
                 for core in range(2):
-                    to = first * 16 + z * 2 + core
-
-                    @pl.when(w != to)
-                    def _():
-                        pltpu.make_async_remote_copy(
-                            src_ref=sb2.at[to], dst_ref=rv2.at[my_t, my_g], send_sem=ssem2,
-                            recv_sem=rsem2.at[my_t], device_id={"wheel": to}, device_id_type=MESH,
-                        ).start()
-
-                    @pl.when(w == to)
-                    def _():
-                        pltpu.make_async_copy(
-                            sb2.at[to], rv2.at[my_t, my_g], rsem2.at[my_t]
-                        ).start()
+                    answer(first * 16 + z * 2 + core, 0)
+
+        left(0)
+        for first in range(2):
+            for z in (7, 4, 5, 6):
+                for core in range(2):
+                    answer(first * 16 + z * 2 + core, 1)
 
     for t in range(2):
         pltpu.make_async_copy(rv2.at[t], rv2.at[t], rsem2.at[t]).wait()
@@ -289,14 +350,18 @@
             lhs, pcv[0, g], (((1,), (1,)), ((), ())), preferred_element_type=F32
         )
 
-    def sent(count, sem):
-        whole = rv1.at[pl.ds(0, count)]
-        pltpu.make_async_copy(whole, whole, sem).wait()
-
     @pl.when(works)
     def _():
         sent(15, ssem1)
-        sent(31, ssem2)
+        mine = lax.rem(w // 8, 2) == 1
+
+        @pl.when(mine)
+        def _():
+            sent(15, ssem2.at[1])
+
+        @pl.when(jnp.logical_not(mine))
+        def _():
+            sent(16, ssem2.at[1])
 
     @pl.when(jnp.logical_not(works))
     def _():
@@ -338,15 +403,20 @@
             pltpu.SemaphoreType.DMA((4,)),
             pltpu.SemaphoreType.DMA,
             pltpu.SemaphoreType.DMA((2,)),
-            pltpu.SemaphoreType.DMA,
+            pltpu.SemaphoreType.DMA((2,)),
             pltpu.SemaphoreType.DMA((2,)),
         ],
         compiler_params=pltpu.CompilerParams(
-            collective_id=0, has_side_effects=True, vmem_limit_bytes=60 * 1024 * 1024
+            collective_id=0, has_side_effects=True, vmem_limit_bytes=40 * 1024 * 1024
         ),
     )(
-        krylov_block, blade_class, neighbors, iface_rows, face_rows, stiffness, lumped_mass,
-        precond, jnp.asarray(kron_table()),
+        *(
+            pltpu.with_memory_space_constraint(operand, pltpu.HBM)
+            for operand in (
+                krylov_block, blade_class, neighbors, iface_rows, face_rows, stiffness, lumped_mass,
+                precond, jnp.asarray(kron_table()),
+            )
+        )
     )
 
 

time: 32.8 us -> 28.2 us (0.86); the launches traced: 32.7 us -> 27.7 us
  Pallas kernels: 31.1 us -> 27 us
  local copies, waits for them, and re-layouts: 1.62 us -> 0.68 us
    pallas_call x1, Pallas kernels: 31.1 us -> 27 us  [on_device(): pl.pallas_call(kernel, out_shape=jax.ShapeDtypeStruct((1, 8, 16, 384), F3...]
    unnamed x1, local copies, waits for them, and re-layouts: 1.62 us -> 0.68 us
where the time goes in v4:
time: 28.2 us; the launch traced here: 27.7 us
  Pallas kernels  27 us (96%)
  local copies, waits for them, and re-layouts  0.68 us (2%)
    pallas_call x1, Pallas kernels, on_device(): pl.pallas_call(kernel, out_shape=jax.ShapeDtypeStruct((1, 8, 16, 384), F3...  27 us
    unnamed x1, local copies, waits for them, and re-layouts  0.68 us

profile of v4, /device:TPU:1, one launch (start us, length us, event | category | flops | bytes accessed | tf_op | source)
XLA Modules:
  0.0 27.7 jit_solution(10569463317247333757)
XLA Ops:
  0.0 27.0 %shard_map.91 = f32[1,8,16,384]{3,2,1,0:T(8,128)S(1)} custom-call(f32[2,2,3,16,256]{4,3,2,1,0:T(8,128)} %kb_hbm.1, s32[2]{0:T(128)} %bc_hbm.1, s32[8,256]{1,0:T(8,128)} %nb_hbm.1, s32[2,64]{1,0:T(2,128)} %ifr_hbm.1, s32[2,64]{1,0:T(2,128)} %fcr_hbm.1, f32[3,3,8,256]{3,2,1,0:T(8,128)} %st_hbm.1, f32[3,256]{1,0:T(4,128)} %ms_hbm.1, ...), custom_call_target="tpu_custom_call" | custom-call | tf_op jit(solution)/shard_map/pallas_call | solution.py:377
  27.0 0.7 %copy.11 = f32[1,8,16,384]{3,2,1,0:T(8,128)} copy(f32[1,8,16,384]{3,2,1,0:T(8,128)S(1)} %shard_map.91) | data formatting | bytes 393216

commit v5 on v4

--- a/solution.py
+++ b/solution.py
@@ -28,7 +28,7 @@
 
 
 def worker_of(t, g):
-    return (g // 4) * 16 + ((7 + g % 4) % 8) * 2 + t
+    return (g // 4) * 16 + (g % 4) * 2 + t
 
 
 def basis_table():
@@ -56,7 +56,7 @@
 
 def kernel(
     kb_hbm, bc_hbm, nb_hbm, ifr_hbm, fcr_hbm, st_hbm, ms_hbm, pc_hbm, km_hbm, out,
-    kb, bc, nb, ifr, fcr, st, ms, pcv, kmv, hs, hsw, hr, hrw, sb, rv1, acc, sb2, rv2,
+    kb, bc, nb, ifr, fcr, st, ms, pcv, kmv, hs, hsw, hr, hrw, sb, rv1, acc, sb2, rv2, hot, base, flip,
     lsem, hsend, hrecv, ssem1, rsem1, ssem2, rsem2,
 ):
     w = lax.axis_index("wheel")
@@ -97,7 +97,7 @@
     greet({"wheel": prv})
 
     my_t = lax.rem(w, 2)
-    along = lax.rem(lax.rem(w // 2, 8) + 1, 8)
+    along = lax.rem(w // 2, 8)
     my_g = (w // 16) * 4 + along
     works = along < 4
 
@@ -210,6 +210,21 @@
         both = jnp.dot(own, one_hot(256, 256, nb[k : k + 1, :]), preferred_element_type=F32)
         ke = stencil(ke, k, both[:96] + both[96:])
 
+    for k in range(8):
+        hot[k] = one_hot(256, 256, nb[k : k + 1, :] - 256)
+    mass = [ms[c : c + 1, :] for c in range(3)]
+    gyro = (-(mass[0] * v[:, 1]), mass[1] * v[:, 0], None)
+    scale = [1.0 + class_step * bc[s].astype(F32) for s in range(2)]
+
+    def scaled(part):
+        return jnp.stack([scale[s] * part[s] for s in range(2)], axis=0)
+
+    for c in range(3):
+        row = -scaled(ke[c]) - shift_value * (mass[c] * v[:, c])
+        if c < 2:
+            row = row - gyro_rate * gyro[c]
+        base[c] = row
+
     @pl.when(has_up)
     def _():
         halos[0].wait_send()
@@ -239,22 +254,10 @@
         axis=0,
     )
     halo = jnp.concatenate((iface, face), axis=1).astype(BF)
+    ke = [jnp.zeros((2, 16, 256), F32) for _ in range(3)]
     for k in range(8):
-        ke = stencil(
-            ke, k, jnp.dot(halo, one_hot(256, 256, nb[k : k + 1, :] - 256), preferred_element_type=F32)
-        )
-
-    mass = [ms[c : c + 1, :] for c in range(3)]
-    gyro = (-(mass[0] * v[:, 1]), mass[1] * v[:, 0], None)
-    rows = []
-    for c in range(3):
-        scaled = jnp.stack(
-            [(1.0 + class_step * bc[s].astype(F32)) * ke[c][s] for s in range(2)], axis=0
-        )
-        row = -scaled - shift_value * (mass[c] * v[:, c])
-        if c < 2:
-            row = row - gyro_rate * gyro[c]
-        rows.append(row)
+        ke = stencil(ke, k, jnp.dot(halo, hot[k], preferred_element_type=F32))
+    rows = [base[c] - scaled(ke[c]) for c in range(3)]
     pack(1, jnp.stack(rows, axis=1))
     send(1)
 
@@ -294,17 +297,6 @@
             @pl.when(w == to)
             def _():
                 pltpu.make_async_copy(sb2.at[to], rv2.at[my_t, my_g], rsem2.at[my_t]).start()
-
-        def left(group):
-            mine = lax.rem(w // 8, 2) == group
-
-            @pl.when(mine)
-            def _():
-                sent(15, ssem2.at[group])
-
-            @pl.when(jnp.logical_not(mine))
-            def _():
-                sent(16, ssem2.at[group])
 
         arrived(0)
         near = field(0)
@@ -321,47 +313,49 @@
                 for core in range(2):
                     answer(first * 16 + z * 2 + core, 0)
 
-        left(0)
+        sent(15, ssem2.at[0])
         for first in range(2):
             for z in (7, 4, 5, 6):
                 for core in range(2):
                     answer(first * 16 + z * 2 + core, 1)
 
-    for t in range(2):
-        pltpu.make_async_copy(rv2.at[t], rv2.at[t], rsem2.at[t]).wait()
     loads[8].wait()
+    for g in range(8):
+        turned = pcv[0, g].T
+        flip[g, 0:96] = turned[96:192]
+        flip[g, 96:192] = turned[288:384]
+
     lane16 = lax.broadcasted_iota(jnp.int32, (16, 128), 1)
+    zero = jnp.zeros((16, 128), F32)
+
+    def placed(t, g, q, at):
+        shift = (at - 32 * (g % 4)) % 128
+        x = rv2[t, g, q].astype(F32)
+        return pltpu.roll(x, shift, 1) if shift else x
+
+    pltpu.make_async_copy(rv2.at[0], rv2.at[0], rsem2.at[0]).wait()
     for g in range(8):
-        turned = []
-        for q in range(2):
-            for t in range(2):
-                x = rv2[t, g, q].astype(F32)
-                shift = (96 * (2 * q + t) - 32 * (g % 4)) % 128
-                turned.append(pltpu.roll(x, shift, 1) if shift else x)
+        low = jnp.where(lane16 < 96, placed(0, g, 0, 0), zero)
+        top = placed(0, g, 1, 64)
         lhs = jnp.concatenate(
-            (
-                jnp.where(lane16 < 96, turned[0], turned[1]),
-                jnp.where(lane16 < 64, turned[1], turned[2]),
-                jnp.where(lane16 < 32, turned[2], turned[3]),
-            ),
-            axis=1,
+            (low, jnp.where(lane16 >= 64, top, zero), jnp.where(lane16 < 32, top, zero)), axis=1
         ).astype(BF)
         out[0, g] = lax.dot_general(
             lhs, pcv[0, g], (((1,), (1,)), ((), ())), preferred_element_type=F32
         )
 
+    pltpu.make_async_copy(rv2.at[1], rv2.at[1], rsem2.at[1]).wait()
+    for g in range(8):
+        top = placed(1, g, 1, 96)
+        lhs = jnp.concatenate(
+            (jnp.where(lane16 < 96, placed(1, g, 0, 0), top), top), axis=1
+        ).astype(BF)
+        out[0, g] += jnp.dot(lhs[:, :192], flip[g], preferred_element_type=F32)
+
     @pl.when(works)
     def _():
         sent(15, ssem1)
-        mine = lax.rem(w // 8, 2) == 1
-
-        @pl.when(mine)
-        def _():
-            sent(15, ssem2.at[1])
-
-        @pl.when(jnp.logical_not(mine))
-        def _():
-            sent(16, ssem2.at[1])
+        sent(16, ssem2.at[1])
 
     @pl.when(jnp.logical_not(works))
     def _():
@@ -398,6 +392,9 @@
             pltpu.VMEM((2, 256, 256), F32),
             pltpu.VMEM((32, 2, 16, 128), BF),
             pltpu.VMEM((2, 8, 2, 16, 128), BF),
+            pltpu.VMEM((8, 256, 256), BF),
+            pltpu.VMEM((3, 2, 16, 256), F32),
+            pltpu.VMEM((8, 192, 384), BF),
             pltpu.SemaphoreType.DMA((9,)),
             pltpu.SemaphoreType.DMA((4,)),
             pltpu.SemaphoreType.DMA((4,)),

time: 28.2 us -> 25.8 us (0.915)
  Pallas kernels: 27 us -> 24.8 us
    pallas_call x1, Pallas kernels: 27 us -> 24.8 us  [on_device(): pl.pallas_call(kernel, out_shape=jax.ShapeDtypeStruct((1, 8, 16, 384), F3...]
where the time goes in v5:
time: 25.8 us; the launch traced here: 25.5 us
  Pallas kernels  24.8 us (96%)
  local copies, waits for them, and re-layouts  0.68 us (3%)
    pallas_call x1, Pallas kernels, on_device(): pl.pallas_call(kernel, out_shape=jax.ShapeDtypeStruct((1, 8, 16, 384), F3...  24.8 us
    unnamed x1, local copies, waits for them, and re-layouts  0.68 us

profile of v5, /device:TPU:1, one launch (start us, length us, event | category | flops | bytes accessed | tf_op | source)
XLA Modules:
  0.0 25.5 jit_solution(1564430194871384429)
XLA Ops:
  0.0 24.8 %shard_map.91 = f32[1,8,16,384]{3,2,1,0:T(8,128)S(1)} custom-call(f32[2,2,3,16,256]{4,3,2,1,0:T(8,128)} %kb_hbm.1, s32[2]{0:T(128)} %bc_hbm.1, s32[8,256]{1,0:T(8,128)} %nb_hbm.1, s32[2,64]{1,0:T(2,128)} %ifr_hbm.1, s32[2,64]{1,0:T(2,128)} %fcr_hbm.1, f32[3,3,8,256]{3,2,1,0:T(8,128)} %st_hbm.1, f32[3,256]{1,0:T(4,128)} %ms_hbm.1, ...), custom_call_target="tpu_custom_call" | custom-call | tf_op jit(solution)/shard_map/pallas_call | solution.py:371
  24.8 0.7 %copy.11 = f32[1,8,16,384]{3,2,1,0:T(8,128)} copy(f32[1,8,16,384]{3,2,1,0:T(8,128)S(1)} %shard_map.91) | data formatting | bytes 393216

commit v6 on v5

--- a/solution.py
+++ b/solution.py
@@ -56,8 +56,8 @@
 
 def kernel(
     kb_hbm, bc_hbm, nb_hbm, ifr_hbm, fcr_hbm, st_hbm, ms_hbm, pc_hbm, km_hbm, out,
-    kb, bc, nb, ifr, fcr, st, ms, pcv, kmv, hs, hsw, hr, hrw, sb, rv1, acc, sb2, rv2, hot, base, flip,
-    lsem, hsend, hrecv, ssem1, rsem1, ssem2, rsem2,
+    kb, bc, nb, ifr, fcr, st, ms, pcv, kmv, hs, hsw, hr, hrw, sb, rv1, acc, sb2, rv2, hot, base, flip, pick_hot,
+    ready, lsem, hsend, hrecv, ssem1, rsem1, ssem2, rsem2,
 ):
     w = lax.axis_index("wheel")
     j = lax.axis_index("slab")
@@ -70,8 +70,9 @@
         pltpu.make_async_copy(src, dst, lsem.at[n])
         for n, (src, dst) in enumerate(
             (
-                (kb_hbm, kb), (ifr_hbm, ifr), (fcr_hbm, fcr), (nb_hbm, nb), (st_hbm, st),
-                (ms_hbm, ms), (bc_hbm, bc), (km_hbm, kmv), (pc_hbm, pcv),
+                (ifr_hbm, ifr), (fcr_hbm, fcr),
+                *((kb_hbm.at[t, p], kb.at[t, p]) for p in range(2) for t in range(2)),
+                (nb_hbm, nb), (st_hbm, st), (ms_hbm, ms), (bc_hbm, bc), (km_hbm, kmv), (pc_hbm, pcv),
             )
         )
     ]
@@ -101,13 +102,29 @@
     my_g = (w // 16) * 4 + along
     works = along < 4
 
+    late = jnp.logical_not(works)
+
     @pl.when(works)
     def _():
-        @pl.loop(1, WHEEL)
+        mine = (w // 16) * 8 + lax.rem(w, 8)
+
+        @pl.loop(1, 16)
         def _(i):
-            greet({"wheel": lax.rem(w + i, WHEEL)})
-
-    for load in loads[:3]:
+            other = lax.rem(mine + i, 16)
+            greet({"wheel": (other // 8) * 16 + lax.rem(other, 8)})
+
+    @pl.when(late)
+    def _():
+        greet({"wheel": w - 2 * jnp.where(along == 7, 7, along - 3)})
+
+    for load in loads[:2]:
+        load.wait()
+    none = jnp.full((1, 64), -1, jnp.int32)
+    index = jnp.concatenate(
+        (ifr[1:2, :], none, none, ifr[0:1, :], fcr[1:2, :], none, none, fcr[0:1, :]), axis=1
+    )
+    pick_hot[...] = one_hot(256, 512, index)
+    for load in loads[2:6]:
         load.wait()
     u = kb[0]
     v = kb[1]
@@ -115,20 +132,29 @@
     ehi = e.astype(BF)
     elo = (e - ehi.astype(F32)).astype(BF)
 
-    none = jnp.full((1, 64), -1, jnp.int32)
-    index = jnp.concatenate(
-        (ifr[1:2, :], none, none, ifr[0:1, :], fcr[1:2, :], none, none, fcr[0:1, :]), axis=1
-    )
-    picks = jnp.dot(ehi, one_hot(256, 512, index), preferred_element_type=F32)
-    hs[0] = picks[:, 0:128].astype(BF)
-    hs[1] = picks[:, 128:256].astype(BF)
+    picks = jnp.dot(ehi, pick_hot[...], preferred_element_type=F32)
+    hs[0] = (picks[0:48, 0:128] + pltpu.roll(picks[48:96, 0:128], 64, 1)).astype(BF)
+    hs[1] = (pltpu.roll(picks[0:48, 128:256], 64, 1) + picks[48:96, 128:256]).astype(BF)
     hsw[0] = picks[48:96, 256:384].astype(BF)
     hsw[1] = picks[0:48, 384:512].astype(BF)
 
+    greeted = 15 + jnp.where(along == 3, 3, 0) + jnp.where(along == 0, 1, 0)
     pl.semaphore_wait(
         barrier,
-        18 + jnp.where(has_up, 1, 0) + jnp.where(has_down, 1, 0) - jnp.where(works, 1, 0),
+        2 + jnp.where(has_up, 1, 0) + jnp.where(has_down, 1, 0) + jnp.where(works, greeted, 0),
     )
+
+    def tell(to):
+        pl.semaphore_signal(ready, inc=1, device_id={"wheel": to}, device_id_type=MESH)
+
+    @pl.when(along == 3)
+    def _():
+        for step in (2, 4, 6):
+            tell(w + step)
+
+    @pl.when(along == 0)
+    def _():
+        tell(w + 14)
 
     halos = [
         pltpu.make_async_remote_copy(
@@ -158,6 +184,20 @@
 
     lane = lax.broadcasted_iota(jnp.int32, (32, 128), 1)
     spot = lane // 32
+
+    def squeeze(a, b, c, d, spare):
+        turned = [pltpu.roll(d, shift, d.ndim - 1) for shift in (96, 64, 32)]
+        return jnp.concatenate(
+            [jnp.where(spare, x, y) for x, y in zip(turned, (a, b, c))], axis=-2
+        )
+
+    def fourth(a, b, c, place, first):
+        axis = a.ndim - 1
+        return jnp.where(
+            place == first,
+            pltpu.roll(a, 32, axis),
+            jnp.where(place == lax.rem(first + 1, 4), pltpu.roll(b, 64, axis), pltpu.roll(c, 96, axis)),
+        )
 
     def pack(t, res):
         for h in range(2):
@@ -168,11 +208,9 @@
                 tile = jnp.where(
                     spot == (g + 1) % 4, one, jnp.where(spot == (g + 2) % 4, two, part[0])
                 )
-                for half in range(2):
-                    rows = jnp.concatenate(
-                        (tile[half * 8 : half * 8 + 8], tile[16 + half * 8 : 24 + half * 8]), axis=0
-                    )
-                    sb[t, h * 4 + g, half] = rows.astype(BF)
+                sb[t, h * 4 + g] = squeeze(
+                    tile[0:8], tile[16:24], tile[8:16], tile[24:32], spot[:8] == (g + 3) % 4
+                ).astype(BF)
 
     slot = lax.rem(w // 8, 2) * 16 + (w // 16) * 8 + lax.rem(w, 8)
     half_sem = rsem1.at[lax.rem(w // 8, 2)]
@@ -193,7 +231,10 @@
                 pltpu.make_async_copy(sb.at[t, g], rv1.at[slot], half_sem).start()
 
     pack(0, v - shift_value * u)
-    send(0)
+
+    @pl.when(works)
+    def _():
+        send(0)
 
     def stencil(ke, k, picked):
         picked = picked.reshape(2, 3, 16, 256)
@@ -202,7 +243,7 @@
                 ke[c] = ke[c] + st[c, d, k : k + 1, :] * picked[:, d]
         return ke
 
-    for load in loads[3:7]:
+    for load in loads[6:10]:
         load.wait()
     own = jnp.concatenate((ehi, elo), axis=0)
     ke = [jnp.zeros((2, 16, 256), F32) for _ in range(3)]
@@ -225,6 +266,11 @@
             row = row - gyro_rate * gyro[c]
         base[c] = row
 
+    @pl.when(late)
+    def _():
+        pl.semaphore_wait(ready, 1)
+        send(0)
+
     @pl.when(has_up)
     def _():
         halos[0].wait_send()
@@ -232,7 +278,7 @@
 
     @pl.when(jnp.logical_not(has_up))
     def _():
-        hr[1] = jnp.zeros((96, 128), BF)
+        hr[1] = jnp.zeros((48, 128), BF)
 
     @pl.when(has_down)
     def _():
@@ -241,11 +287,19 @@
 
     @pl.when(jnp.logical_not(has_down))
     def _():
-        hr[0] = jnp.zeros((96, 128), BF)
+        hr[0] = jnp.zeros((48, 128), BF)
 
     halos[2].wait()
     halos[3].wait()
-    iface = hr[0].astype(F32) + hr[1].astype(F32)
+    lower, upper = hr[0].astype(F32), hr[1].astype(F32)
+    left_half = lax.broadcasted_iota(jnp.int32, (48, 128), 1) < 64
+    iface = jnp.concatenate(
+        (
+            jnp.where(left_half, lower, pltpu.roll(upper, 64, 1)),
+            jnp.where(left_half, pltpu.roll(lower, 64, 1), upper),
+        ),
+        axis=0,
+    )
     face = jnp.concatenate(
         (
             hrw[0].astype(F32) + picks[48:96, 384:512],
@@ -267,12 +321,21 @@
 
     @pl.when(works)
     def _():
-        loads[7].wait()
+        loads[10].wait()
+
+        corner = lax.rem(my_g, 4)
+        place = lax.broadcasted_iota(jnp.int32, (16, 8, 128), 2) // 32
 
         def field(part):
-            both = rv1[part * 16 : part * 16 + 16]
+            got = rv1[part * 16 : part * 16 + 16].astype(F32)
+            a, b, c = (got[:, n * 8 : n * 8 + 8] for n in range(3))
+            d = fourth(a, b, c, place, corner)
             return jnp.concatenate(
-                (both[:, 0].reshape(256, 128), both[:, 1].reshape(256, 128)), axis=1
+                [
+                    jnp.concatenate(pair, axis=1).astype(BF).reshape(256, 128)
+                    for pair in ((a, b), (c, d))
+                ],
+                axis=1,
             )
 
         def transform(first, part, data):
@@ -306,10 +369,11 @@
         far = field(1)
         for first in range(2):
             har = (acc[first] + transform(first, 1, far)).reshape(16, 2, 8, 256)
-            sb2[first * 16 : first * 16 + 16] = jnp.concatenate(
-                (har[..., :128], har[..., 128:]), axis=2
+            sb2[first * 16 : first * 16 + 16] = squeeze(
+                har[:, 0, :, :128], har[:, 0, :, 128:], har[:, 1, :, :128], har[:, 1, :, 128:],
+                place == lax.rem(corner + 3, 4),
             ).astype(BF)
-            for z in range(4):
+            for z in (0, 1, 2, 3):
                 for core in range(2):
                     answer(first * 16 + z * 2 + core, 0)
 
@@ -319,7 +383,7 @@
                 for core in range(2):
                     answer(first * 16 + z * 2 + core, 1)
 
-    loads[8].wait()
+    loads[11].wait()
     for g in range(8):
         turned = pcv[0, g].T
         flip[g, 0:96] = turned[96:192]
@@ -330,7 +394,12 @@
 
     def placed(t, g, q, at):
         shift = (at - 32 * (g % 4)) % 128
-        x = rv2[t, g, q].astype(F32)
+        got = rv2[t, g].astype(F32)
+        if q == 0:
+            x = got[:16]
+        else:
+            last = fourth(got[:8], got[8:16], got[16:], lane16[:8] // 32, g % 4)
+            x = jnp.concatenate((got[16:], last), axis=0)
         return pltpu.roll(x, shift, 1) if shift else x
 
     pltpu.make_async_copy(rv2.at[0], rv2.at[0], rsem2.at[0]).wait()
@@ -357,9 +426,9 @@
         sent(15, ssem1)
         sent(16, ssem2.at[1])
 
-    @pl.when(jnp.logical_not(works))
-    def _():
-        loads[7].wait()
+    @pl.when(late)
+    def _():
+        loads[10].wait()
         sent(16, ssem1)
 
 
@@ -383,19 +452,21 @@
             pltpu.VMEM((3, 256), F32),
             pltpu.VMEM((1, 8, 384, 384), BF),
             pltpu.VMEM((2, 512, 512), BF),
-            pltpu.VMEM((2, 96, 128), BF),
             pltpu.VMEM((2, 48, 128), BF),
-            pltpu.VMEM((2, 96, 128), BF),
             pltpu.VMEM((2, 48, 128), BF),
-            pltpu.VMEM((2, 8, 2, 16, 128), BF),
-            pltpu.VMEM((32, 2, 16, 128), BF),
+            pltpu.VMEM((2, 48, 128), BF),
+            pltpu.VMEM((2, 48, 128), BF),
+            pltpu.VMEM((2, 8, 24, 128), BF),
+            pltpu.VMEM((32, 24, 128), BF),
             pltpu.VMEM((2, 256, 256), F32),
-            pltpu.VMEM((32, 2, 16, 128), BF),
-            pltpu.VMEM((2, 8, 2, 16, 128), BF),
+            pltpu.VMEM((32, 24, 128), BF),
+            pltpu.VMEM((2, 8, 24, 128), BF),
             pltpu.VMEM((8, 256, 256), BF),
             pltpu.VMEM((3, 2, 16, 256), F32),
             pltpu.VMEM((8, 192, 384), BF),
-            pltpu.SemaphoreType.DMA((9,)),
+            pltpu.VMEM((256, 512), BF),
+            pltpu.SemaphoreType.REGULAR,
+            pltpu.SemaphoreType.DMA((12,)),
             pltpu.SemaphoreType.DMA((4,)),
             pltpu.SemaphoreType.DMA((4,)),
             pltpu.SemaphoreType.DMA,

time: 25.8 us -> 25.3 us (0.981)
  Pallas kernels: 24.8 us -> 24.2 us
    pallas_call x1, Pallas kernels: 24.8 us -> 24.2 us  [on_device(): pl.pallas_call(kernel, out_shape=jax.ShapeDtypeStruct((1, 8, 16, 384), F3...]
where the time goes in v6:
time: 25.3 us; the launch traced here: 24.9 us
  Pallas kernels  24.2 us (96%)
  local copies, waits for them, and re-layouts  0.68 us (3%)
    pallas_call x1, Pallas kernels, on_device(): pl.pallas_call(kernel, out_shape=jax.ShapeDtypeStruct((1, 8, 16, 384), F3...  24.2 us
    unnamed x1, local copies, waits for them, and re-layouts  0.68 us

profile of v6, /device:TPU:1, one launch (start us, length us, event | category | flops | bytes accessed | tf_op | source)
XLA Modules:
  0.0 24.9 jit_solution(7494771982779452586)
XLA Ops:
  0.0 24.2 %shard_map.91 = f32[1,8,16,384]{3,2,1,0:T(8,128)S(1)} custom-call(f32[2,2,3,16,256]{4,3,2,1,0:T(8,128)} %kb_hbm.1, s32[2]{0:T(128)} %bc_hbm.1, s32[8,256]{1,0:T(8,128)} %nb_hbm.1, s32[2,64]{1,0:T(2,128)} %ifr_hbm.1, s32[2,64]{1,0:T(2,128)} %fcr_hbm.1, f32[3,3,8,256]{3,2,1,0:T(8,128)} %st_hbm.1, f32[3,256]{1,0:T(4,128)} %ms_hbm.1, ...), custom_call_target="tpu_custom_call" | custom-call | tf_op jit(solution)/shard_map/pallas_call | solution.py:440
  24.2 0.7 %copy.11 = f32[1,8,16,384]{3,2,1,0:T(8,128)} copy(f32[1,8,16,384]{3,2,1,0:T(8,128)S(1)} %shard_map.91) | data formatting | bytes 393216

commit v7 on v6

--- a/solution.py
+++ b/solution.py
@@ -216,8 +216,9 @@
     half_sem = rsem1.at[lax.rem(w // 8, 2)]
 
     def send(t):
-        for g in range(8):
-            to = worker_of(t, g)
+        for n in range(8):
+            g = lax.rem(n + 4 * (1 - w // 16), 8)
+            to = (g // 4) * 16 + (n % 4) * 2 + t
 
             @pl.when(w != to)
             def _():
@@ -315,6 +316,12 @@
     pack(1, jnp.stack(rows, axis=1))
     send(1)
 
+    loads[11].wait()
+    for g in range(8):
+        turned = pcv[0, g].T
+        for n, part in enumerate((0, 2, 1, 3)):
+            flip[g, n * 96 : n * 96 + 96] = turned[part * 96 : part * 96 + 96]
+
     def sent(count, sem):
         whole = rv1.at[pl.ds(0, count)]
         pltpu.make_async_copy(whole, whole, sem).wait()
@@ -379,18 +386,11 @@
 
         sent(15, ssem2.at[0])
         for first in range(2):
-            for z in (7, 4, 5, 6):
+            for z in (6, 5, 7, 4):
                 for core in range(2):
                     answer(first * 16 + z * 2 + core, 1)
 
-    loads[11].wait()
-    for g in range(8):
-        turned = pcv[0, g].T
-        flip[g, 0:96] = turned[96:192]
-        flip[g, 96:192] = turned[288:384]
-
     lane16 = lax.broadcasted_iota(jnp.int32, (16, 128), 1)
-    zero = jnp.zeros((16, 128), F32)
 
     def placed(t, g, q, at):
         shift = (at - 32 * (g % 4)) % 128
@@ -402,24 +402,22 @@
             x = jnp.concatenate((got[16:], last), axis=0)
         return pltpu.roll(x, shift, 1) if shift else x
 
+    def product(t, g):
+        top = placed(t, g, 1, 96)
+        lhs = jnp.concatenate(
+            (jnp.where(lane16 < 96, placed(t, g, 0, 0), top), top), axis=1
+        ).astype(BF)
+        return jnp.dot(
+            lhs[:, :192], flip[g, t * 192 : t * 192 + 192], preferred_element_type=F32
+        )
+
     pltpu.make_async_copy(rv2.at[0], rv2.at[0], rsem2.at[0]).wait()
     for g in range(8):
-        low = jnp.where(lane16 < 96, placed(0, g, 0, 0), zero)
-        top = placed(0, g, 1, 64)
-        lhs = jnp.concatenate(
-            (low, jnp.where(lane16 >= 64, top, zero), jnp.where(lane16 < 32, top, zero)), axis=1
-        ).astype(BF)
-        out[0, g] = lax.dot_general(
-            lhs, pcv[0, g], (((1,), (1,)), ((), ())), preferred_element_type=F32
-        )
+        out[0, g] = product(0, g)
 
     pltpu.make_async_copy(rv2.at[1], rv2.at[1], rsem2.at[1]).wait()
     for g in range(8):
-        top = placed(1, g, 1, 96)
-        lhs = jnp.concatenate(
-            (jnp.where(lane16 < 96, placed(1, g, 0, 0), top), top), axis=1
-        ).astype(BF)
-        out[0, g] += jnp.dot(lhs[:, :192], flip[g], preferred_element_type=F32)
+        out[0, g] += product(1, g)
 
     @pl.when(works)
     def _():
@@ -463,7 +461,7 @@
             pltpu.VMEM((2, 8, 24, 128), BF),
             pltpu.VMEM((8, 256, 256), BF),
             pltpu.VMEM((3, 2, 16, 256), F32),
-            pltpu.VMEM((8, 192, 384), BF),
+            pltpu.VMEM((8, 384, 384), BF),
             pltpu.VMEM((256, 512), BF),
             pltpu.SemaphoreType.REGULAR,
             pltpu.SemaphoreType.DMA((12,)),

time: 25.3 us -> 24.5 us (0.968)
  Pallas kernels: 24.2 us -> 23.4 us
    pallas_call x1, Pallas kernels: 24.2 us -> 23.4 us  [on_device(): pl.pallas_call(kernel, out_shape=jax.ShapeDtypeStruct((1, 8, 16, 384), F3...]
where the time goes in v7:
time: 24.5 us; the launch traced here: 24.1 us
  Pallas kernels  23.4 us (96%)
  local copies, waits for them, and re-layouts  0.68 us (3%)
    pallas_call x1, Pallas kernels, on_device(): pl.pallas_call(kernel, out_shape=jax.ShapeDtypeStruct((1, 8, 16, 384), F3...  23.4 us
    unnamed x1, local copies, waits for them, and re-layouts  0.68 us

profile of v7, /device:TPU:1, one launch (start us, length us, event | category | flops | bytes accessed | tf_op | source)
XLA Modules:
  0.0 24.1 jit_solution(17095581462365797281)
XLA Ops:
  0.0 23.4 %shard_map.91 = f32[1,8,16,384]{3,2,1,0:T(8,128)S(1)} custom-call(f32[2,2,3,16,256]{4,3,2,1,0:T(8,128)} %kb_hbm.1, s32[2]{0:T(128)} %bc_hbm.1, s32[8,256]{1,0:T(8,128)} %nb_hbm.1, s32[2,64]{1,0:T(2,128)} %ifr_hbm.1, s32[2,64]{1,0:T(2,128)} %fcr_hbm.1, f32[3,3,8,256]{3,2,1,0:T(8,128)} %st_hbm.1, f32[3,256]{1,0:T(4,128)} %ms_hbm.1, ...), custom_call_target="tpu_custom_call" | custom-call | tf_op jit(solution)/shard_map/pallas_call | solution.py:438
  23.4 0.7 %copy.11 = f32[1,8,16,384]{3,2,1,0:T(8,128)} copy(f32[1,8,16,384]{3,2,1,0:T(8,128)S(1)} %shard_map.91) | data formatting | bytes 393216

commit v8 on v7

--- a/solution.py
+++ b/solution.py
@@ -103,6 +103,9 @@
     works = along < 4
 
     late = jnp.logical_not(works)
+    side = (w < 16)
+    relayed = late & side
+    direct = late & jnp.logical_not(side)
 
     @pl.when(works)
     def _():
@@ -113,7 +116,11 @@
             other = lax.rem(mine + i, 16)
             greet({"wheel": (other // 8) * 16 + lax.rem(other, 8)})
 
-    @pl.when(late)
+        @pl.loop(0, 8)
+        def _(i):
+            greet({"wheel": 24 + i})
+
+    @pl.when(relayed)
     def _():
         greet({"wheel": w - 2 * jnp.where(along == 7, 7, along - 3)})
 
@@ -130,7 +137,6 @@
     v = kb[1]
     e = (u + damping_ratio * v).reshape(96, 256)
     ehi = e.astype(BF)
-    elo = (e - ehi.astype(F32)).astype(BF)
 
     picks = jnp.dot(ehi, pick_hot[...], preferred_element_type=F32)
     hs[0] = (picks[0:48, 0:128] + pltpu.roll(picks[48:96, 0:128], 64, 1)).astype(BF)
@@ -138,21 +144,21 @@
     hsw[0] = picks[48:96, 256:384].astype(BF)
     hsw[1] = picks[0:48, 384:512].astype(BF)
 
-    greeted = 15 + jnp.where(along == 3, 3, 0) + jnp.where(along == 0, 1, 0)
+    told = jnp.where(along == 3, 3, 0) + jnp.where(along == 0, 1, 0)
+    greeted = jnp.where(works, 15 + jnp.where(side, told, 0), jnp.where(direct, 16, 0))
     pl.semaphore_wait(
-        barrier,
-        2 + jnp.where(has_up, 1, 0) + jnp.where(has_down, 1, 0) + jnp.where(works, greeted, 0),
+        barrier, 2 + jnp.where(has_up, 1, 0) + jnp.where(has_down, 1, 0) + greeted
     )
 
     def tell(to):
         pl.semaphore_signal(ready, inc=1, device_id={"wheel": to}, device_id_type=MESH)
 
-    @pl.when(along == 3)
+    @pl.when(side & (along == 3))
     def _():
         for step in (2, 4, 6):
             tell(w + step)
 
-    @pl.when(along == 0)
+    @pl.when(side & (along == 0))
     def _():
         tell(w + 14)
 
@@ -233,7 +239,7 @@
 
     pack(0, v - shift_value * u)
 
-    @pl.when(works)
+    @pl.when(works | direct)
     def _():
         send(0)
 
@@ -246,6 +252,7 @@
 
     for load in loads[6:10]:
         load.wait()
+    elo = (e - ehi.astype(F32)).astype(BF)
     own = jnp.concatenate((ehi, elo), axis=0)
     ke = [jnp.zeros((2, 16, 256), F32) for _ in range(3)]
     for k in range(8):
@@ -267,7 +274,7 @@
             row = row - gyro_rate * gyro[c]
         base[c] = row
 
-    @pl.when(late)
+    @pl.when(relayed)
     def _():
         pl.semaphore_wait(ready, 1)
         send(0)

time: 24.5 us -> 24.3 us (level); the launches traced: 24.1 us -> 24.2 us
  no operation moved by 1% of the time
where the time goes in v8:
time: 24.3 us; the launch traced here: 24.2 us
  Pallas kernels  23.5 us (97%)
  local copies, waits for them, and re-layouts  0.68 us (3%)
    pallas_call x1, Pallas kernels, on_device(): pl.pallas_call(kernel, out_shape=jax.ShapeDtypeStruct((1, 8, 16, 384), F3...  23.5 us
    unnamed x1, local copies, waits for them, and re-layouts  0.68 us

profile of v8, /device:TPU:1, one launch (start us, length us, event | category | flops | bytes accessed | tf_op | source)
XLA Modules:
  0.0 24.2 jit_solution(1547144320231182079)
XLA Ops:
  0.0 23.5 %shard_map.91 = f32[1,8,16,384]{3,2,1,0:T(8,128)S(1)} custom-call(f32[2,2,3,16,256]{4,3,2,1,0:T(8,128)} %kb_hbm.1, s32[2]{0:T(128)} %bc_hbm.1, s32[8,256]{1,0:T(8,128)} %nb_hbm.1, s32[2,64]{1,0:T(2,128)} %ifr_hbm.1, s32[2,64]{1,0:T(2,128)} %fcr_hbm.1, f32[3,3,8,256]{3,2,1,0:T(8,128)} %st_hbm.1, f32[3,256]{1,0:T(4,128)} %ms_hbm.1, ...), custom_call_target="tpu_custom_call" | custom-call | tf_op jit(solution)/shard_map/pallas_call | solution.py:445
  23.5 0.7 %copy.11 = f32[1,8,16,384]{3,2,1,0:T(8,128)} copy(f32[1,8,16,384]{3,2,1,0:T(8,128)S(1)} %shard_map.91) | data formatting | bytes 393216

commit v9 on v8

--- a/solution.py
+++ b/solution.py
@@ -387,13 +387,13 @@
                 har[:, 0, :, :128], har[:, 0, :, 128:], har[:, 1, :, :128], har[:, 1, :, 128:],
                 place == lax.rem(corner + 3, 4),
             ).astype(BF)
-            for z in (0, 1, 2, 3):
+            for z in (0, 1, 6, 2, 3):
                 for core in range(2):
                     answer(first * 16 + z * 2 + core, 0)
 
-        sent(15, ssem2.at[0])
+        sent(19, ssem2.at[0])
         for first in range(2):
-            for z in (6, 5, 7, 4):
+            for z in (5, 7, 4):
                 for core in range(2):
                     answer(first * 16 + z * 2 + core, 1)
 
@@ -429,7 +429,7 @@
     @pl.when(works)
     def _():
         sent(15, ssem1)
-        sent(16, ssem2.at[1])
+        sent(12, ssem2.at[1])
 
     @pl.when(late)
     def _():

time: 24.3 us -> 24.3 us (level)
  no operation moved by 1% of the time
where the time goes in v9:
time: 24.3 us; the launch traced here: 24.2 us
  Pallas kernels  23.5 us (97%)
  local copies, waits for them, and re-layouts  0.68 us (3%)
    pallas_call x1, Pallas kernels, on_device(): pl.pallas_call(kernel, out_shape=jax.ShapeDtypeStruct((1, 8, 16, 384), F3...  23.5 us
    unnamed x1, local copies, waits for them, and re-layouts  0.68 us

profile of v9, /device:TPU:1, one launch (start us, length us, event | category | flops | bytes accessed | tf_op | source)
XLA Modules:
  0.0 24.2 jit_solution(16301363144415406742)
XLA Ops:
  0.0 23.5 %shard_map.91 = f32[1,8,16,384]{3,2,1,0:T(8,128)S(1)} custom-call(f32[2,2,3,16,256]{4,3,2,1,0:T(8,128)} %kb_hbm.1, s32[2]{0:T(128)} %bc_hbm.1, s32[8,256]{1,0:T(8,128)} %nb_hbm.1, s32[2,64]{1,0:T(2,128)} %ifr_hbm.1, s32[2,64]{1,0:T(2,128)} %fcr_hbm.1, f32[3,3,8,256]{3,2,1,0:T(8,128)} %st_hbm.1, f32[3,256]{1,0:T(4,128)} %ms_hbm.1, ...), custom_call_target="tpu_custom_call" | custom-call | tf_op jit(solution)/shard_map/pallas_call | solution.py:445
  23.5 0.7 %copy.11 = f32[1,8,16,384]{3,2,1,0:T(8,128)} copy(f32[1,8,16,384]{3,2,1,0:T(8,128)S(1)} %shard_map.91) | data formatting | bytes 393216

commit v10 on v8

--- a/solution.py
+++ b/solution.py
@@ -393,7 +393,7 @@
 
         sent(15, ssem2.at[0])
         for first in range(2):
-            for z in (6, 5, 7, 4):
+            for z in (5, 6, 7, 4):
                 for core in range(2):
                     answer(first * 16 + z * 2 + core, 1)
 

time: 24.3 us -> 24.3 us (level)
  no operation moved by 1% of the time
where the time goes in v10:
time: 24.3 us; the launch traced here: 24.2 us
  Pallas kernels  23.5 us (97%)
  local copies, waits for them, and re-layouts  0.68 us (3%)
    pallas_call x1, Pallas kernels, on_device(): pl.pallas_call(kernel, out_shape=jax.ShapeDtypeStruct((1, 8, 16, 384), F3...  23.5 us
    unnamed x1, local copies, waits for them, and re-layouts  0.68 us

profile of v10, /device:TPU:1, one launch (start us, length us, event | category | flops | bytes accessed | tf_op | source)
XLA Modules:
  0.0 24.2 jit_solution(6734407574469769941)
XLA Ops:
  0.0 23.5 %shard_map.91 = f32[1,8,16,384]{3,2,1,0:T(8,128)S(1)} custom-call(f32[2,2,3,16,256]{4,3,2,1,0:T(8,128)} %kb_hbm.1, s32[2]{0:T(128)} %bc_hbm.1, s32[8,256]{1,0:T(8,128)} %nb_hbm.1, s32[2,64]{1,0:T(2,128)} %ifr_hbm.1, s32[2,64]{1,0:T(2,128)} %fcr_hbm.1, f32[3,3,8,256]{3,2,1,0:T(8,128)} %st_hbm.1, f32[3,256]{1,0:T(4,128)} %ms_hbm.1, ...), custom_call_target="tpu_custom_call" | custom-call | tf_op jit(solution)/shard_map/pallas_call | solution.py:445
  23.5 0.7 %copy.11 = f32[1,8,16,384]{3,2,1,0:T(8,128)} copy(f32[1,8,16,384]{3,2,1,0:T(8,128)S(1)} %shard_map.91) | data formatting | bytes 393216
